TPU v7x, 32 devices: a whole 2x2x4 slice. The times are simulated.
32 devices in a mesh: seq: 16 (over z, y, x), mdl: 2 (over core).
Axes of the slice: x: 2, y: 2, z: 4, core: 2. Of those that a mesh axis runs over, the one named last changes fastest.
Arguments:
- hidden_in: bfloat16 [32, 4, 2048], P(None, None, 'seq'), may hold values from -25 to 25
- cache_keys: bfloat16 [32, 512, 2048], P(None, 'seq', 'mdl'), may hold values from -250 to 250, as said below
- cache_values: bfloat16 [32, 512, 2048], P(None, 'seq', 'mdl'), may hold values from -6 to 6
- lengths: int32 [32], replicated, may hold values from 1 to 508, as said below
- query_weight: bfloat16 [2048, 2048], P('seq', 'mdl'), may hold values from -0.125 to 0.125
- key_weight: bfloat16 [2048, 2048], P('seq', 'mdl'), may hold values from -0.125 to 0.125
- value_weight: bfloat16 [2048, 2048], P('seq', 'mdl'), may hold values from -0.125 to 0.125
- out_weight: bfloat16 [2048, 2048], P('mdl', 'seq'), may hold values from -0.125 to 0.125
- gate_weight: bfloat16 [2048, 8192], P('seq', 'mdl'), may hold values from -0.125 to 0.125
- up_weight: bfloat16 [2048, 8192], P('seq', 'mdl'), may hold values from -0.125 to 0.125
- down_weight: bfloat16 [8192, 2048], P('mdl', 'seq'), may hold values from -0.0625 to 0.0625
Outputs:
- hidden_out: bfloat16 [32, 4, 2048], P(None, None, 'seq')
- new_cache_keys: bfloat16 [32, 512, 2048], P(None, 'seq', 'mdl')
- new_cache_values: bfloat16 [32, 512, 2048], P(None, 'seq', 'mdl')
Inputs may be any that keep to these rules, and one draw needn't show every extreme that they name: `cache_keys`: keys are stored after their rotary embedding. `lengths`: at least one request has exactly 508 cached positions.
All inputs are finite; a program needn't handle non-finite values.
Results may differ from a plain program's by a relative error of at most 0.012.
The roundings to bfloat16 on the way count: a program that leaves them out, or rounds other values in their place, can miss the bound.
Values may be sent and summed in bfloat16 or wider, within the bound.
A program may use at most 64 MiB of HBM per device.

v0:
```python
import math

import jax
import jax.numpy as jnp
from jax import lax
from jax.sharding import PartitionSpec as P

D = 2048
HEADS = 16


EPS = 1e-05
THETA = 10000.0
NEGATIVE = -1e30


def rotate(vectors, placed_pos):
    head_size = vectors.shape[-1]
    half_dim = head_size // 2
    freqs = THETA ** (-jnp.arange(half_dim, dtype=jnp.float32) * 2.0 / head_size)
    angles = placed_pos.astype(jnp.float32)[..., None, None] * freqs
    cosine = jnp.cos(angles)
    sine = jnp.sin(angles)
    first_half = vectors[..., :half_dim]
    second_half = vectors[..., half_dim:]
    return jnp.concatenate(
        [first_half * cosine - second_half * sine, second_half * cosine + first_half * sine],
        axis=-1,
    )


def normalize(widened, row_sums, square_sums):
    row_mean = row_sums / D
    second_moment = square_sums / D
    inverse = 1.0 / jnp.sqrt(second_moment - row_mean * row_mean + EPS)
    return ((widened - row_mean[..., None]) * inverse[..., None]).astype(jnp.bfloat16)


def body(
    hidden_in,
    cache_keys,
    cache_values,
    lengths,
    query_weight,
    key_weight,
    value_weight,
    out_weight,
    gate_weight,
    up_weight,
    down_weight,
):
    requests, token_count, narrow_width = hidden_in.shape
    slot_count = cache_keys.shape[1]
    local_width = cache_keys.shape[2]
    head_size = D // HEADS
    local_heads = local_width // head_size
    score_scale = 1.0 / math.sqrt(head_size)
    shard_index = lax.axis_index("seq")
    slot_ids = shard_index * slot_count + jnp.arange(slot_count, dtype=jnp.int32)
    live_slots = slot_ids[None, :] < lengths[:, None]
    old_keys = cache_keys.reshape(requests, slot_count, local_heads, head_size)
    old_values = cache_values.reshape(requests, slot_count, local_heads, head_size).astype(
        jnp.float32
    )
    positions = lengths[:, None] + jnp.arange(token_count, dtype=jnp.int32)[None, :]
    out_list = []
    key_list = []
    value_list = []
    for token_step in range(token_count):
        row_block = hidden_in[:, token_step : token_step + 1]
        block_rows = row_block.shape[1]
        widened = row_block.astype(jnp.float32)
        row_sums, square_sums = lax.psum(
            (jnp.sum(widened, axis=-1), jnp.sum(widened * widened, axis=-1)), "seq"
        )
        normed = normalize(widened, row_sums, square_sums)
        query_part = jnp.einsum(
            "rnc,cm->rnm", normed, query_weight, preferred_element_type=jnp.float32
        )
        key_part = jnp.einsum("rnc,cm->rnm", normed, key_weight, preferred_element_type=jnp.float32)
        value_part = jnp.einsum(
            "rnc,cm->rnm", normed, value_weight, preferred_element_type=jnp.float32
        )
        queries, keys_full, values_full = lax.psum((query_part, key_part, value_part), "seq")
        placed_pos = positions[:, token_step : token_step + block_rows]
        queries = rotate(
            queries.reshape(requests, block_rows, local_heads, head_size), placed_pos
        ).astype(jnp.bfloat16)
        new_key = rotate(
            keys_full.reshape(requests, block_rows, local_heads, head_size), placed_pos
        ).astype(jnp.bfloat16)
        new_value = values_full.reshape(requests, block_rows, local_heads, head_size).astype(
            jnp.bfloat16
        )
        keys_new = jnp.concatenate(key_list + [new_key], axis=1)
        values_new = jnp.concatenate(value_list + [new_value], axis=1)
        old_scores = (
            jnp.einsum("rnhd,rjhd->rnhj", queries, old_keys, preferred_element_type=jnp.float32)
            * score_scale
        )
        old_scores = jnp.where(live_slots[:, None, None, :], old_scores, NEGATIVE)
        top_old = jnp.max(old_scores, axis=-1)
        weights_old = jnp.where(
            live_slots[:, None, None, :], jnp.exp(old_scores - top_old[..., None]), 0.0
        )
        total_old = jnp.sum(weights_old, axis=-1)
        summed_old = jnp.einsum(
            "rnhj,rjhd->rnhd", weights_old, old_values, precision=lax.Precision.HIGHEST
        )
        top_cache = lax.pmax(top_old, "seq")
        factor_old = jnp.exp(top_old - top_cache)
        total_cache, summed_cache = lax.psum(
            (total_old * factor_old, summed_old * factor_old[..., None]), "seq"
        )
        new_scores = (
            jnp.einsum("rnhd,rshd->rnhs", queries, keys_new, preferred_element_type=jnp.float32)
            * score_scale
        )
        key_index = jnp.arange(keys_new.shape[1], dtype=jnp.int32)
        query_index = token_step + jnp.arange(block_rows, dtype=jnp.int32)
        allowed = key_index[None, :] <= query_index[:, None]
        new_scores = jnp.where(allowed[None, :, None, :], new_scores, NEGATIVE)
        top_new = jnp.max(new_scores, axis=-1)
        weights_new = jnp.exp(new_scores - top_new[..., None])
        total_new = jnp.sum(weights_new, axis=-1)
        summed_new = jnp.einsum(
            "rnhs,rshd->rnhd",
            weights_new,
            values_new.astype(jnp.float32),
            precision=lax.Precision.HIGHEST,
        )
        top_score = jnp.maximum(top_cache, top_new)
        factor_cache = jnp.exp(top_cache - top_score)
        factor_new = jnp.exp(top_new - top_score)
        running = total_cache * factor_cache + total_new * factor_new
        combined = summed_cache * factor_cache[..., None] + summed_new * factor_new[..., None]
        attended = (
            (combined / running[..., None])
            .astype(jnp.bfloat16)
            .reshape(requests, block_rows, local_width)
        )
        attn_part = jnp.einsum(
            "rnm,mc->rnc", attended, out_weight, preferred_element_type=jnp.float32
        )
        mixed = widened + lax.psum(attn_part, "mdl")
        sums_mixed, squares_mixed = lax.psum(
            (jnp.sum(mixed, axis=-1), jnp.sum(mixed * mixed, axis=-1)), "seq"
        )
        normed2 = normalize(mixed, sums_mixed, squares_mixed)
        gate_part = jnp.einsum(
            "rnc,cf->rnf", normed2, gate_weight, preferred_element_type=jnp.float32
        )
        up_part = jnp.einsum("rnc,cf->rnf", normed2, up_weight, preferred_element_type=jnp.float32)
        gate_full, up_full = lax.psum((gate_part, up_part), "seq")
        act_full = (jax.nn.silu(gate_full) * up_full).astype(jnp.bfloat16)
        down_part = jnp.einsum(
            "rnf,fc->rnc", act_full, down_weight, preferred_element_type=jnp.float32
        )
        block_out = (mixed + lax.psum(down_part, "mdl")).astype(jnp.bfloat16)
        block_out, new_key, new_value = (block_out, new_key, new_value)
        out_list.append(block_out)
        key_list.append(new_key)
        value_list.append(new_value)
    hidden_out = jnp.concatenate(out_list, axis=1)
    keys_all = jnp.concatenate(key_list, axis=1)
    values_all = jnp.concatenate(value_list, axis=1)
    slot_hits = slot_ids[None, None, :] == positions[:, :, None]
    one_hot = slot_hits.astype(jnp.bfloat16)
    written = jnp.any(slot_hits, axis=1)[..., None]
    placed_keys = jnp.einsum(
        "rts,rtm->rsm",
        one_hot,
        keys_all.reshape(requests, token_count, local_width),
        preferred_element_type=jnp.float32,
    ).astype(jnp.bfloat16)
    placed_values = jnp.einsum(
        "rts,rtm->rsm",
        one_hot,
        values_all.reshape(requests, token_count, local_width),
        preferred_element_type=jnp.float32,
    ).astype(jnp.bfloat16)
    new_cache_keys = jnp.where(written, placed_keys, cache_keys)
    new_cache_values = jnp.where(written, placed_values, cache_values)
    return (hidden_out, new_cache_keys, new_cache_values)


def solution(mesh):
    placed = (
        P(None, None, "seq"),
        P(None, "seq", "mdl"),
        P(None, "seq", "mdl"),
        P(),
        P("seq", "mdl"),
        P("seq", "mdl"),
        P("seq", "mdl"),
        P("mdl", "seq"),
        P("seq", "mdl"),
        P("seq", "mdl"),
        P("mdl", "seq"),
    )
    return jax.shard_map(
        body,
        mesh=mesh,
        in_specs=placed,
        out_specs=(P(None, None, "seq"), P(None, "seq", "mdl"), P(None, "seq", "mdl")),
        check_vma=False,
    )
```

profile of v0, /device:TPU:0, one launch (start us, length us, event | category | flops | bytes accessed | tf_op | source)
XLA Modules:
  0.0 663.0 jit_solution(5343042440964158596)
XLA Ops:
  7.2 1.0 fusion.177
  8.5 43.5 %all-reduce.2 = (f32[32,1]{0,1:T(1,128)S(1)}, f32[32,1]{0,1:T(1,128)S(1)}, f32[32,1]{0,1:T(1,128)S(1)}, f32[32,1]{0,1:T(1,128)S(1)}, f32[32,1]{0,1:T(1,128)S(1)}...) all-reduce(f32[32,1]{0,1:T(1,128)S(1)} %bitcast.640, ...), channel_id=1, replica_groups=mesh['seq'=16,'mdl'=2] {'seq'}, use_global_device_ids=true, to_apply=%region_67.68 | all-reduce | flops 256 | bytes 2048 | tf_op jit(solution)/shard_map/psum | solution.py:73
  52.0 1.2 convolution_bitcast_fusion.10
  53.9 1.2 convolution_bitcast_fusion.19
  55.8 1.2 convolution_bitcast_fusion.16
  63.4 100.4 %all-reduce.20.cloned.1.call-done = (f32[32,1,8,128]{3,2,0,1:T(8,128)}, f32[32,1,8,128]{3,2,0,1:T(8,128)}, f32[32,1,8,128]{3,2,0,1:T(8,128)}, f32[32,1,8,128]{3,2,0,1:T(8,128)}) async-done(((f32[32,1,8,128]{3,2,0,1:T(8,128)}, f32[32,1,8,128]{3,2,0,1:T(8,128)}, f32[32,1,8,128]{3,2,0,1:T(8,128)}, f32[32,1,8,128]{3,2,0,1:T(8,128)}), (f32[32,1,8,128]{3,2,0,1:T(8,128)}, f32[32,1,8,128]{3,2,0,1:T(8,128)}, ...) | async-done | bytes 524304 | tf_op jit(solution)/shard_map/psum | solution.py:84
  163.8 1.2 fusion.71
  165.2 2.8 fusion.14
  168.2 1.2 fusion.12
  169.6 1.2 fusion.10
  171.0 1.2 fusion.8
  172.9 1.8 fusion
  174.6 1.8 fusion.2
  176.4 1.8 fusion.4
  178.2 1.8 fusion.6
  179.9 75.1 %all-reduce.6 = (f32[32,1,8]{2,0,1:T(8,128)S(1)}, f32[32,1,8]{2,0,1:T(8,128)S(1)}, f32[32,1,8]{2,0,1:T(8,128)S(1)}, f32[32,1,8]{2,0,1:T(8,128)S(1)}) all-reduce(f32[32,1,8]{2,0,1:T(8,128)S(1)} %bitcast.619, f32[32,1,8]{2,0,1:T(8,128)S(1)} %bitcast.618, f32[32,1,8]{2,0,1:T(8,128)S(1)} %bitcast.617, ...), channel_id=1, replica_groups=mesh['seq'=16,'mdl'=2] {'seq'}, use_global_device_ids=true, to_apply=%region_70.71 | all-reduce | flops 1024 | bytes 8192 | tf_op jit(solution)/shard_map/pmax | solution.py:110
  255.1 0.7 multiply_bitcast_fusion
  255.8 0.8 multiply_bitcast_fusion.1
  256.6 0.7 multiply_bitcast_fusion.2
  257.3 0.8 multiply_bitcast_fusion.3
  258.4 81.7 %all-reduce.25 = (bf16[32,1,1024]{2,0,1:T(8,128)(2,1)S(1)}, bf16[32,1,1024]{2,0,1:T(8,128)(2,1)S(1)}, bf16[32,1,1024]{2,0,1:T(8,128)(2,1)S(1)}, bf16[32,1,1024]{...) all-reduce(f32[32,1,1024]{2,0,1:T(8,128)S(1)} %convolution_bitcast_, ...), channel_id=1, replica_groups=mesh['seq'=16,'mdl'=2] {'seq'}, use_global_device_ids=true, to_apply=%region_74.75 | all-reduce | flops 132096 | bytes 794624 | tf_op jit(solution)/shard_map/psum | solution.py:84
  340.5 29.7 %all-reduce.18.cloned.1.call-done = (f32[32,1,8,128]{3,2,0,1:T(8,128)}, f32[32,1,8,128]{3,2,0,1:T(8,128)}, f32[32,1,8,128]{3,2,0,1:T(8,128)}, f32[32,1,8,128]{3,...) async-done(((f32[32,1,8,128]{3,2,0,1:T(8,128)}, f32[32,1,8,128]{3,2,0,1:T(8,128)}, ...) | async-done | bytes 1048592 | tf_op jit(solution)/shard_map/psum | solution.py:84
  370.1 1.1 multiply_subtract_fusion
  371.2 1.1 multiply_subtract_fusion.1
  372.3 1.1 multiply_subtract_fusion.2
  373.5 1.1 multiply_subtract_fusion.3
  379.1 0.8 copy.38
  379.8 1.1 fusion.36
  380.9 0.8 fusion.145
  381.9 0.8 convolution_bitcast_fusion.21
  382.7 1.0 fusion.40
  383.7 0.7 fusion.147
  384.6 0.8 convolution_bitcast_fusion.23
  385.6 1.0 fusion.55
  386.7 0.8 fusion.149
  387.7 0.8 convolution_bitcast_fusion.25
  388.7 0.7 fusion.151
  389.6 0.8 convolution_bitcast_fusion.27
  390.5 17.2 %all-reduce.24.cloned.1.call-done = (f32[32,1,128]{2,0,1:T(8,128)}, f32[32,1,128]{2,0,1:T(8,128)}, f32[32,1,128]{2,0,1:T(8,128)}, f32[32,1,128]{2,0,1:T(8,128)}) async-done(((f32[32,1,128]{2,0,1:T(8,128)}, f32[32,1,128]{2,0,1:T(8,128)}, f32[32,1,128]{2,0,1:T(8,128)}, f32[32,1,128]{2,0,1:T(8,128)}), (f32[32,1,128]{2,0,1:T(8,128)}, f32[32,1,128]{2,0,1:T(8,128)}, f32[32,1,128]{2,0,1:T(8,128)}, ...) | async-done | bytes 65552 | tf_op jit(solution)/shard_map/psum | solution.py:145
  407.7 0.8 fusion.155
  408.5 0.8 fusion.154
  409.3 0.8 fusion.153
  410.2 0.8 fusion.152
  411.0 42.0 %all-reduce = (f32[32,1]{0,1:T(1,128)S(1)}, f32[32,1]{0,1:T(1,128)S(1)}, f32[32,1]{0,1:T(1,128)S(1)}, f32[32,1]{0,1:T(1,128)S(1)}, f32[32,1]{0,1:T(1,128)S(1)}, ...) all-reduce(f32[32,1]{0,1:T(1,128)S(1)} %bitcast.648, ...), channel_id=1, replica_groups=mesh['seq'=16,'mdl'=2] {'seq'}, use_global_device_ids=true, to_apply=%region_82.83 | all-reduce | flops 256 | bytes 2048 | tf_op jit(solution)/shard_map/psum | solution.py:146
  453.0 0.8 fusion.131
  453.8 1.1 convolution_bitcast_fusion
  454.9 1.1 convolution_bitcast_fusion.1
  456.1 1.1 convolution_bitcast_fusion.2
  457.2 1.1 convolution_bitcast_fusion.3
  458.3 1.1 convolution_bitcast_fusion.4
  459.4 1.1 convolution_bitcast_fusion.5
  460.6 1.1 convolution_bitcast_fusion.6
  461.7 1.1 convolution_bitcast_fusion.7
  463.0 0.9 copy.42
  463.9 0.8 compare_reduce_fusion
  464.7 1.0 pad_maximum_fusion.2
  465.7 3.3 convert_select_fusion
  469.1 161.2 %all-reduce.16.cloned.1.call-done = (f32[32,1,4096]{2,0,1:T(8,128)}, f32[32,1,4096]{2,0,1:T(8,128)}, f32[32,1,4096]{2,0,1:T(8,128)}, f32[32,1,4096]{2,0,1:T(8,12...) async-done(((f32[32,1,4096]{2,0,1:T(8,128)}, f32[32,1,4096]{2,0,1:T(8,128)}, f32[32,1,4096]{2,0,1:T(8,128)}, ...) | async-done | bytes 4194320 | tf_op jit(solution)/shard_map/psum | solution.py:154
  630.3 2.6 convolution_bitcast_fusion.20
  632.9 0.9 convolution_bitcast_fusion.22
  634.1 0.9 convolution_bitcast_fusion.24
  635.1 0.9 convolution_bitcast_fusion.26
  636.1 3.7 convert_select_fusion.1
  639.7 13.2 %all-reduce.22.cloned.1.call-done = (f32[32,1,128]{2,0,1:T(8,128)}, f32[32,1,128]{2,0,1:T(8,128)}, f32[32,1,128]{2,0,1:T(8,128)}, f32[32,1,128]{2,0,1:T(8,128)}) async-done(((f32[32,1,128]{2,0,1:T(8,128)}, f32[32,1,128]{2,0,1:T(8,128)}, f32[32,1,128]{2,0,1:T(8,128)}, f32[32,1,128]{2,0,1:T(8,128)}), (f32[32,1,128]{2,0,1:T(8,128)}, f32[32,1,128]{2,0,1:T(8,128)}, f32[32,1,128]{2,0,1:T(8,128)}, ...) | async-done | bytes 65552 | tf_op jit(solution)/shard_map/psum | solution.py:159
  (206 shorter events, 20.2 us)
Async XLA Ops:
  7.2 446.6 %copy-start = (bf16[128,4096]{1,0:T(8,128)(2,1)S(1)}, bf16[128,4096]{1,0:T(8,128)(2,1)}, u32[]{:S(2)}) copy-start(bf16[128,4096]{1,0:T(8,128)(2,1)} %param.20) | copy-start | bytes 3145732
  7.2 50.5 %copy-start.2 = (bf16[128,1024]{1,0:T(8,128)(2,1)S(1)}, bf16[128,1024]{1,0:T(8,128)(2,1)}, u32[]{:S(2)}) copy-start(bf16[128,1024]{1,0:T(8,128)(2,1)} %param.15) | copy-start | bytes 786436
  7.2 51.5 %copy-start.3 = (bf16[128,1024]{1,0:T(8,128)(2,1)S(1)}, bf16[128,1024]{1,0:T(8,128)(2,1)}, u32[]{:S(2)}) copy-start(bf16[128,1024]{1,0:T(8,128)(2,1)} %param.16) | copy-start | bytes 786436
  7.2 156.6 %all-reduce.20.cloned.1.call-start = ((), (), s32[]{:S(2)}) async-start(), calls=%async_computation.2 | async-start | bytes 1048576 | tf_op jit(solution)/shard_map/psum | solution.py:84
  53.9 5.7 copy-start.4
  58.6 4.4 copy-start.37
  58.6 311.6 %all-reduce.18.cloned.1.call-start = ((), (), s32[]{:S(2)}) async-start(), calls=%async_computation.1 | async-start | bytes 2097152 | tf_op jit(solution)/shard_map/psum | solution.py:84
  62.9 102.1 %copy-start.32 = (s32[32,4]{0,1:T(4,128)}, s32[32,4]{0,1:T(4,128)S(1)}, u32[]{:S(2)}) copy-start(s32[32,4]{0,1:T(4,128)S(1)} %iota_add_fusion) | copy-start | bytes 1540
  63.0 102.1 %copy-start.35 = (s32[32]{0:T(128)}, s32[32]{0:T(128)S(1)}, u32[]{:S(2)}) copy-start(s32[32]{0:T(128)S(1)} %iota_add_fusion.1) | copy-start | bytes 388
  163.8 4.1 copy-start.10
  163.8 4.4 copy-start.38
  167.9 1.4 copy-start.9
  168.2 2.6 copy-start.23
  169.3 1.4 copy-start.8
  169.6 2.6 copy-start.25
  171.0 1.8 copy-start.27
  171.0 1.8 copy-start.6
  255.0 3.4 copy-start.30
  258.1 149.5 %all-reduce.24.cloned.1.call-start = ((), (), s32[]{:S(2)}) async-start(), calls=%async_computation.4 | async-start | bytes 131072 | tf_op jit(solution)/shard_map/psum | solution.py:145
  340.2 34.7 %copy-start.11 = (bf16[32,1,1024]{2,0,1:T(8,128)(2,1)}, bf16[32,1,1024]{2,0,1:T(8,128)(2,1)S(1)}, u32[]{:S(2)}) copy-start(bf16[32,1,1024]{2,0,1:T(8,128)(2,1)S(1)} %get-tuple-element.40) | copy-start | bytes 196612
  340.2 34.7 %copy-start.12 = (bf16[32,1,1024]{2,0,1:T(8,128)(2,1)}, bf16[32,1,1024]{2,0,1:T(8,128)(2,1)S(1)}, u32[]{:S(2)}) copy-start(bf16[32,1,1024]{2,0,1:T(8,128)(2,1)S(1)} %get-tuple-element.41) | copy-start | bytes 196612
  340.2 43.5 %copy-start.13 = (bf16[32,1,1024]{2,0,1:T(8,128)(2,1)}, bf16[32,1,1024]{2,0,1:T(8,128)(2,1)S(1)}, u32[]{:S(2)}) copy-start(bf16[32,1,1024]{2,0,1:T(8,128)(2,1)S(1)} %get-tuple-element.42) | copy-start | bytes 196612
  340.3 34.7 %copy-start.28 = (bf16[32,8,128,1]{2,1,0,3:T(8,128)(2,1)S(1)}, bf16[32,8,128,1]{2,1,0,3:T(8,128)(2,1)}, u32[]{:S(2)}) copy-start(bf16[32,8,128,1]{2,1,0,3:T(8,128)(2,1)} %copy-done.27) | copy-start | bytes 196612
  372.3 3.5 copy-start.26
  375.0 2.3 copy-start.24
  375.9 5.8 copy-start.22
  376.3 5.6 copy-start.5
  377.3 7.2 %copy-start.21 = (f32[32,1,8,128]{3,2,0,1:T(8,128)S(1)}, f32[32,1,8,128]{3,2,0,1:T(8,128)}, u32[]{:S(2)}) copy-start(f32[32,1,8,128]{3,2,0,1:T(8,128)} %get-tuple-element.69) | copy-start | bytes 393220
  380.9 5.8 copy-start.29
  380.9 6.6 copy-start.20
  382.7 6.0 copy-start.31
  382.7 6.7 %copy-start.19 = (f32[32,1,8,128]{3,2,0,1:T(8,128)S(1)}, f32[32,1,8,128]{3,2,0,1:T(8,128)}, u32[]{:S(2)}) copy-start(f32[32,1,8,128]{3,2,0,1:T(8,128)} %get-tuple-element.71) | copy-start | bytes 393220
  386.6 68.2 %copy-start.1 = (bf16[128,4096]{1,0:T(8,128)(2,1)S(1)}, bf16[128,4096]{1,0:T(8,128)(2,1)}, u32[]{:S(2)}) copy-start(bf16[128,4096]{1,0:T(8,128)(2,1)} %param.19) | copy-start | bytes 3145732
  390.4 239.9 %all-reduce.16.cloned.1.call-start = ((), (), s32[]{:S(2)}) async-start(), calls=%async_computation | async-start | bytes 8388608 | tf_op jit(solution)/shard_map/psum | solution.py:154
  407.7 48.3 %copy-start.16 = (f32[32,1,128]{2,0,1:T(8,128)S(1)}, f32[32,1,128]{2,0,1:T(8,128)}, u32[]{:S(2)}) copy-start(f32[32,1,128]{2,0,1:T(8,128)} %get-tuple-element.85) | copy-start | bytes 49156
  454.9 3.4 copy-start.15
  457.2 3.3 copy-start.14
  462.7 3.0 copy-start.7
  462.8 190.2 %all-reduce.22.cloned.1.call-start = ((), (), s32[]{:S(2)}) async-start(), calls=%async_computation.3 | async-start | bytes 131072 | tf_op jit(solution)/shard_map/psum | solution.py:159
  464.7 1.0 copy-start.33
  469.0 163.9 %copy-start.39 = (bf16[4096,128]{1,0:T(8,128)(2,1)S(1)}, bf16[4096,128]{1,0:T(8,128)(2,1)}, u32[]{:S(2)}) copy-start(bf16[4096,128]{1,0:T(8,128)(2,1)} %param.21) | copy-start | bytes 3145732
  630.3 2.6 copy-start.44
  630.3 2.6 copy-start.45
  632.9 1.0 copy-start.42
  632.9 1.2 copy-start.43
  633.8 1.2 copy-start.40
  633.8 1.3 copy-start.41
  635.0 1.0 copy-start.34
  635.0 1.0 copy-start.36
  636.0 16.9 %copy-start.18 = (f32[32,1,128]{2,0,1:T(8,128)S(1)}, f32[32,1,128]{2,0,1:T(8,128)}, u32[]{:S(2)}) copy-start(f32[32,1,128]{2,0,1:T(8,128)} %get-tuple-element.84) | copy-start | bytes 49156
  636.1 17.6 %copy-start.17 = (f32[32,1,128]{2,0,1:T(8,128)S(1)}, f32[32,1,128]{2,0,1:T(8,128)}, u32[]{:S(2)}) copy-start(f32[32,1,128]{2,0,1:T(8,128)} %get-tuple-element.85) | copy-start | bytes 49156
Sparse Core Ops, SparseCore 0:
  58.7 105.0 all-reduce.19
  258.2 111.8 all-reduce.17
  390.5 17.0 all-reduce.23
  462.9 167.3 all-reduce.15
  636.1 16.7 all-reduce.21
where the time goes:
time: 665 us; the launch traced here: 663 us
  waiting for transfers between devices  322 us (48%)
  blocking collectives  242 us (36%)
  matrix products  47.1 us (7%)
  other arithmetic  25.5 us (4%)
  between operations  14.6 us (2%)
  local copies, waits for them, and re-layouts  11.3 us (2%)
    psum x1, waiting for transfers between devices, body(): gate_full, up_full = lax.psum((gate_part, up_part), 'seq')  161 us
    psum x2, waiting for transfers between devices, body(): lax.psum((query_part, key_part, value_part), 'seq')  130 us
    psum x1, blocking collectives, body(): lax.psum((query_part, key_part, value_part), 'seq')  81.7 us
    pmax x1, blocking collectives, body(): top_cache = lax.pmax(top_old, 'seq')  75.1 us
    psum x1, blocking collectives, body(): lax.psum((jnp.sum(widened, axis=-1), jnp.sum(widened * widened, axis=-1))...  43.5 us
    psum x1, blocking collectives, body(): lax.psum((jnp.sum(mixed, axis=-1), jnp.sum(mixed * mixed, axis=-1)), 'seq')  42 us
    psum x1, waiting for transfers between devices, body(): mixed = widened + lax.psum(attn_part, 'mdl')  17.2 us
  transfers between devices with their start and end apart: 5, of which 5 were waited for; matrix products, arithmetic and copies ran while one was open for 2% of the time, Pallas kernels for 0%

commit v1 on v0

--- a/solution.py
+++ b/solution.py
@@ -66,8 +66,8 @@
     out_list = []
     key_list = []
     value_list = []
-    for token_step in range(token_count):
-        row_block = hidden_in[:, token_step : token_step + 1]
+    for token_step in range(1):
+        row_block = hidden_in
         block_rows = row_block.shape[1]
         widened = row_block.astype(jnp.float32)
         row_sums, square_sums = lax.psum(

time: 665 us -> 623 us (0.937)
  matrix products: 47.1 us -> 31 us
  other arithmetic: 25.5 us -> 9.96 us
    psum x2 -> x1, waiting for transfers between devices: 130 us -> 102 us  [body(): lax.psum((query_part, key_part, value_part), 'seq')]
    psum x0 -> x1, waiting for transfers between devices: none -> 27.1 us  [body(): lax.psum((total_old * factor_old, summed_old * factor_old[..., None]), 's...]
where the time goes in v1:
time: 623 us; the launch traced here: 622 us
  waiting for transfers between devices  319 us (51%)
  blocking collectives  243 us (39%)
  matrix products  31 us (5%)
  between operations  14.1 us (2%)
  other arithmetic  9.96 us (2%)
    psum x1, waiting for transfers between devices, body(): gate_full, up_full = lax.psum((gate_part, up_part), 'seq')  160 us
    psum x1, waiting for transfers between devices, body(): lax.psum((query_part, key_part, value_part), 'seq')  102 us
    psum x1, blocking collectives, body(): lax.psum((query_part, key_part, value_part), 'seq')  82 us
    pmax x1, blocking collectives, body(): top_cache = lax.pmax(top_old, 'seq')  75.7 us
    psum x1, blocking collectives, body(): lax.psum((jnp.sum(widened, axis=-1), jnp.sum(widened * widened, axis=-1))...  43.5 us
    psum x1, blocking collectives, body(): lax.psum((jnp.sum(mixed, axis=-1), jnp.sum(mixed * mixed, axis=-1)), 'seq')  42 us
    psum x1, waiting for transfers between devices, body(): lax.psum((total_old * factor_old, summed_old * factor_old[..., None]), 's...  27.1 us
    psum x1, waiting for transfers between devices, body(): mixed = widened + lax.psum(attn_part, 'mdl')  16.7 us
  transfers between devices with their start and end apart: 5, of which 5 were waited for; matrix products, arithmetic and copies ran while one was open for 2% of the time, Pallas kernels for 0%

profile of v1, /device:TPU:0, one launch (start us, length us, event | category | flops | bytes accessed | tf_op | source)
XLA Modules:
  0.0 622.2 jit_solution(543046160231867355)
XLA Ops:
  7.2 0.0 copy-start
  7.2 0.0 copy-start.1
  7.2 0.0 all-reduce.12.cloned.1.call-start
  7.2 1.0 convert_reduce_fusion
  8.2 43.5 %all-reduce.2 = (f32[32,4]{0,1:T(4,128)S(1)}, f32[32,4]{0,1:T(4,128)S(1)}) all-reduce(f32[32,4]{0,1:T(4,128)S(1)} %get-tuple-element.12, f32[32,4]{0,1:T(4,128)S(1)} %get-tuple-element.11), channel_id=1, replica_groups=mesh['seq'=16,'mdl'=2] {'seq'}, use_global_device_ids=true, to_apply=%region_3.0 | all-reduce | flops 256 | bytes 2048 | tf_op jit(solution)/shard_map/psum | solution.py:73
  51.7 1.2 fusion.42
  53.0 0.1 copy.35
  53.1 0.0 copy-start.18
  53.1 1.1 copy.23
  54.2 0.0 all-reduce.12.cloned.1.call-update
  54.2 0.0 all-reduce.20.cloned.1.call-start
  54.3 0.3 fusion.40
  54.6 0.1 copy.36
  54.7 1.1 copy.26
  55.8 0.1 broadcast_compare_fusion
  55.9 0.1 iota_add_fusion
  56.0 0.5 multiply_cosine_fusion
  56.5 102.0 %all-reduce.12.cloned.1.call-done = f32[32,4,8,128]{3,1,2,0:T(4,128)} async-done(((f32[32,4,8,128]{3,1,2,0:T(4,128)}), f32[32,4,8,128]{3,1,2,0:T(4,128)}) %all-reduce.12.cloned.1.call-update) | async-done | bytes 524304 | tf_op jit(solution)/shard_map/psum | solution.py:84
  158.5 1.7 subtract_convert_fusion
  160.2 0.0 copy-start.15
  160.2 0.0 copy-start.17
  160.3 0.0 copy-start.2
  160.3 4.0 fusion.71
  164.2 0.0 copy-done.11
  164.2 75.7 %pmax.7 = f32[32,4,8]{1,2,0:T(8,128)S(1)} all-reduce(f32[32,4,8]{1,2,0:T(8,128)S(1)} %get-tuple-element.40), channel_id=1, replica_groups=mesh['seq'=16,'mdl'=2] {'seq'}, use_global_device_ids=true, to_apply=%region_6.0 | all-reduce | flops 1024 | bytes 8192 | tf_op jit(solution)/shard_map/pmax | solution.py:110
  240.0 1.7 fusion.34
  241.7 0.7 fusion.70
  242.4 3.7 fusion.9
  246.1 0.0 all-reduce.20.cloned.1.call-update
  246.1 0.0 all-reduce.14.cloned.1.call-start
  246.2 1.3 fusion.38
  247.4 82.0 %all-reduce.21 = (bf16[32,4,1024]{2,0,1:T(8,128)(2,1)S(1)}, f32[32,4,8]{1,2,0:T(8,128)S(1)}) all-reduce(f32[32,4,1024]{2,0,1:T(8,128)S(1)} %fusion.38, f32[32,4,8]{1,2,0:T(8,128)} %get-tuple-element.26), channel_id=1, replica_groups=mesh['seq'=16,'mdl'=2] {'seq'}, use_global_device_ids=true, to_apply=%region_10.11 | all-reduce | flops 132096 | bytes 794624 | tf_op jit(solution)/shard_map/psum | solution.py:84
  329.5 27.1 %all-reduce.20.cloned.1.call-done = (f32[32,4,8,128]{3,1,2,0:T(4,128)}, f32[32,4,8,128]{3,1,2,0:T(4,128)}) async-done(((f32[32,4,8,128]{3,1,2,0:T(4,128)}, f32[32,4,8,128]{3,1,2,0:T(4,128)}), (f32[32,4,8,128]{3,1,2,0:T(4,128)}, f32[32,4,8,128]{3,1,2,0:T(4,128)})) %all-reduce.20.cloned.1.call-update) | async-done | bytes 1048592 | tf_op jit(solution)/shard_map/psum | solution.py:112
  356.7 0.0 copy-done.10
  356.7 1.7 multiply_subtract_fusion
  358.4 2.1 fusion.72
  360.5 0.4 fusion.33
  361.0 0.1 multiply_add_fusion.1
  361.0 0.0 copy-done.19
  361.1 0.0 copy-start.14
  361.1 2.1 fusion.26
  363.2 0.1 reshape.140
  363.3 0.0 copy-done.14
  363.3 0.0 copy-start.6
  363.3 0.8 fusion.36
  364.2 0.0 all-reduce.14.cloned.1.call-update
  364.2 0.0 all-reduce.18.cloned.1.call-start
  364.3 16.7 %all-reduce.14.cloned.1.call-done = f32[32,4,128]{2,0,1:T(8,128)} async-done(((f32[32,4,128]{2,0,1:T(8,128)}), f32[32,4,128]{2,0,1:T(8,128)}) %all-reduce.14.cloned.1.call-update) | async-done | bytes 65552 | tf_op jit(solution)/shard_map/psum | solution.py:145
  381.0 1.0 fusion.67
  382.0 42.0 %all-reduce = (f32[32,4]{0,1:T(4,128)S(1)}, f32[32,4]{0,1:T(4,128)S(1)}) all-reduce(f32[32,4]{0,1:T(4,128)S(1)} %get-tuple-element.10, f32[32,4]{0,1:T(4,128)S(1)} %get-tuple-element.9), channel_id=1, replica_groups=mesh['seq'=16,'mdl'=2] {'seq'}, use_global_device_ids=true, to_apply=%region_18.19 | all-reduce | flops 256 | bytes 2048 | tf_op jit(solution)/shard_map/psum | solution.py:146
  424.0 2.6 fusion.29
  426.6 1.8 fusion.31
  428.4 0.0 all-reduce.18.cloned.1.call-update
  428.5 0.0 all-reduce.16.cloned.1.call-start
  428.5 0.1 compare_reduce_fusion
  428.6 1.5 copy-done.3
  430.1 3.6 convert_select_fusion
  433.7 159.6 %all-reduce.18.cloned.1.call-done = (f32[32,4,4096]{2,0,1:T(8,128)}, f32[32,4,4096]{2,0,1:T(8,128)}) async-done(((f32[32,4,4096]{2,0,1:T(8,128)}, f32[32,4,4096]{2,0,1:T(8,128)}), (f32[32,4,4096]{2,0,1:T(8,128)}, f32[32,4,4096]{2,0,1:T(8,128)})) %all-reduce.18.cloned.1.call-update) | async-done | bytes 4194320 | tf_op jit(solution)/shard_map/psum | solution.py:154
  593.3 4.0 fusion.27
  597.3 0.0 all-reduce.16.cloned.1.call-update
  597.3 3.5 convert_select_fusion.1
  600.8 13.3 %all-reduce.16.cloned.1.call-done = f32[32,4,128]{2,0,1:T(8,128)} async-done(((f32[32,4,128]{2,0,1:T(8,128)}), f32[32,4,128]{2,0,1:T(8,128)}) %all-reduce.16.cloned.1.call-update) | async-done | bytes 65552 | tf_op jit(solution)/shard_map/psum | solution.py:159
  614.2 0.9 add_convert_fusion.1
  615.0 0.6 copy.31
  (34 shorter events, 0.2 us)
Async XLA Ops:
  7.2 416.8 %copy-start = (bf16[128,4096]{1,0:T(8,128)(2,1)S(1)}, bf16[128,4096]{1,0:T(8,128)(2,1)}, u32[]{:S(2)}) copy-start(bf16[128,4096]{1,0:T(8,128)(2,1)} %param.20) | copy-start | bytes 3145732
  7.2 47.1 %copy-start.1 = (bf16[32,4,128]{2,1,0:T(4,128)(2,1)S(1)}, bf16[32,4,128]{2,1,0:T(4,128)(2,1)}, u32[]{:S(2)}) copy-start(bf16[32,4,128]{2,1,0:T(4,128)(2,1)} %param.11) | copy-start | bytes 98308
  7.2 47.1 %copy-start.13 = (bf16[128,1024]{1,0:T(8,128)(2,1)S(1)}, bf16[128,1024]{1,0:T(8,128)(2,1)}, u32[]{:S(2)}) copy-start(bf16[128,1024]{1,0:T(8,128)(2,1)} %param.16) | copy-start | bytes 786436
  7.2 151.3 %all-reduce.12.cloned.1.call-start = ((), (), s32[]{:S(2)}) async-start(), calls=%async_computation | async-start | bytes 1048576 | tf_op jit(solution)/shard_map/psum | solution.py:84
  53.1 2.8 copy-start.18
  54.2 302.4 %all-reduce.20.cloned.1.call-start = ((), (), s32[]{:S(2)}) async-start(), calls=%async_computation.4 | async-start | bytes 2097152 | tf_op jit(solution)/shard_map/psum | solution.py:112
  56.5 107.7 %copy-start.9 = (f32[32,4,64]{2,1,0:T(4,128)}, f32[32,4,64]{2,1,0:T(4,128)S(1)}, u32[]{:S(2)}) copy-start(f32[32,4,64]{2,1,0:T(4,128)S(1)} %get-tuple-element.32) | copy-start | bytes 98308
  56.5 107.7 %copy-start.11 = (f32[32,4,64]{2,1,0:T(4,128)}, f32[32,4,64]{2,1,0:T(4,128)S(1)}, u32[]{:S(2)}) copy-start(f32[32,4,64]{2,1,0:T(4,128)S(1)} %get-tuple-element.33) | copy-start | bytes 98308
  160.2 4.0 copy-start.15
  160.2 4.0 copy-start.17
  160.3 82.1 %copy-start.2 = (bf16[32,32,1024]{2,1,0:T(8,128)(2,1)S(1)}, bf16[32,32,1024]{2,1,0:T(8,128)(2,1)}, u32[]{:S(2)}) copy-start(bf16[32,32,1024]{2,1,0:T(8,128)(2,1)} %param.13) | copy-start | bytes 6291460
  246.1 110.6 %copy-start.10 = (f32[32,4,64]{2,1,0:T(4,128)S(1)}, f32[32,4,64]{2,1,0:T(4,128)}, u32[]{:S(2)}) copy-start(f32[32,4,64]{2,1,0:T(4,128)} %copy-done.9) | copy-start | bytes 98308
  246.1 110.6 %copy-start.12 = (f32[32,4,64]{2,1,0:T(4,128)S(1)}, f32[32,4,64]{2,1,0:T(4,128)}, u32[]{:S(2)}) copy-start(f32[32,4,64]{2,1,0:T(4,128)} %copy-done.11) | copy-start | bytes 98308
  246.1 112.3 %copy-start.16 = (bf16[32,4,8,64]{3,1,2,0:T(4,128)(2,1)S(1)}, bf16[32,4,8,64]{3,1,2,0:T(4,128)(2,1)}, u32[]{:S(2)}) copy-start(bf16[32,4,8,64]{3,1,2,0:T(4,128)(2,1)} %copy-done.15) | copy-start | bytes 393220
  246.1 134.9 %all-reduce.14.cloned.1.call-start = ((), (), s32[]{:S(2)}) async-start(), calls=%async_computation.1 | async-start | bytes 131072 | tf_op jit(solution)/shard_map/psum | solution.py:145
  329.5 33.6 %copy-start.8 = (bf16[32,4,1024]{2,0,1:T(8,128)(2,1)}, bf16[32,4,1024]{2,0,1:T(8,128)(2,1)S(1)}, u32[]{:S(2)}) copy-start(bf16[32,4,1024]{2,0,1:T(8,128)(2,1)S(1)} %get-tuple-element.15) | copy-start | bytes 786436
  358.4 4.8 copy-start.7
  358.4 2.7 copy-start.19
  361.1 2.3 copy-start.14
  363.3 63.3 %copy-start.6 = (bf16[128,4096]{1,0:T(8,128)(2,1)S(1)}, bf16[128,4096]{1,0:T(8,128)(2,1)}, u32[]{:S(2)}) copy-start(bf16[128,4096]{1,0:T(8,128)(2,1)} %param.19) | copy-start | bytes 3145732
  364.2 229.1 %all-reduce.18.cloned.1.call-start = ((), (), s32[]{:S(2)}) async-start(), calls=%async_computation.3 | async-start | bytes 8388608 | tf_op jit(solution)/shard_map/psum | solution.py:154
  381.0 45.7 %copy-start.5 = (f32[32,4,128]{2,0,1:T(8,128)S(1)}, f32[32,4,128]{2,0,1:T(8,128)}, u32[]{:S(2)}) copy-start(f32[32,4,128]{2,0,1:T(8,128)} %all-reduce.14.cloned.1.call-done) | copy-start | bytes 196612
  428.4 1.7 copy-start.3
  428.5 185.7 %all-reduce.16.cloned.1.call-start = ((), (), s32[]{:S(2)}) async-start(), calls=%async_computation.2 | async-start | bytes 131072 | tf_op jit(solution)/shard_map/psum | solution.py:159
  593.3 4.0 copy-start.4
Sparse Core Ops, SparseCore 0:
  54.3 104.1 all-reduce.11
  246.2 110.4 all-reduce.19
  364.3 16.5 all-reduce.13
  428.6 164.7 all-reduce.17
  597.4 16.6 all-reduce.15

commit v2 on v1

--- a/solution.py
+++ b/solution.py
@@ -1,8 +1,11 @@
+import functools
 import math
 
 import jax
 import jax.numpy as jnp
 from jax import lax
+from jax.experimental import pallas as pl
+from jax.experimental.pallas import tpu as pltpu
 from jax.sharding import PartitionSpec as P
 
 D = 2048
@@ -36,7 +39,7 @@
     return ((widened - row_mean[..., None]) * inverse[..., None]).astype(jnp.bfloat16)
 
 
-def body(
+def body_plain(
     hidden_in,
     cache_keys,
     cache_values,
@@ -184,6 +187,494 @@
     return (hidden_out, new_cache_keys, new_cache_values)
 
 
+PLANE = 4
+MESH = pl.DeviceIdType.MESH
+F32 = jnp.float32
+BF16 = jnp.bfloat16
+
+
+def plane_peer(me, j):
+    p = me % PLANE
+    x, y = p % 2, p // 2
+    if j % 2:
+        x = 1 - x
+    if j // 2:
+        y = 1 - y
+    return (me // PLANE) * PLANE + y * 2 + x
+
+
+def depth_peer(me, k, depth):
+    return ((me // PLANE + k) % depth) * PLANE + me % PLANE
+
+
+def remote(src, dst, send, recv, device):
+    copy = pltpu.make_async_remote_copy(
+        src_ref=src, dst_ref=dst, send_sem=send, recv_sem=recv, device_id=device, device_id_type=MESH
+    )
+    copy.start()
+    return copy
+
+
+def wait_all(copies):
+    for copy in copies:
+        copy.wait()
+
+
+def enter(n, me, partner=None):
+    barrier = pltpu.get_barrier_semaphore()
+    for k in range(1, n):
+        pl.semaphore_signal(
+            barrier, inc=1, device_id={"seq": (me + k) % n}, device_id_type=MESH
+        )
+    if partner is not None:
+        pl.semaphore_signal(barrier, inc=1, device_id={"mdl": partner}, device_id_type=MESH)
+    pl.semaphore_wait(barrier, n - 1 + (partner is not None))
+
+
+def share_small(n, me, slots, send, recv):
+    wait_all(
+        [
+            remote(
+                slots.at[me], slots.at[me], send.at[k - 1], recv.at[k - 1], {"seq": (me + k) % n}
+            )
+            for k in range(1, n)
+        ]
+    )
+
+
+def scatter_sum(n, me, part, got_plane, half, got_depth, sems):
+    depth = n // PLANE
+    z, p = me // PLANE, me % PLANE
+    copies = []
+    for j in range(1, PLANE):
+        peer = plane_peer(me, j)
+        copies.append(
+            remote(
+                part.at[:, peer % PLANE],
+                got_plane.at[j - 1],
+                sems[0].at[j - 1],
+                sems[1].at[j - 1],
+                {"seq": peer},
+            )
+        )
+    wait_all(copies)
+    for d in range(depth):
+        total = part[d, p].astype(F32)
+        for j in range(PLANE - 1):
+            total = total + got_plane[j, d].astype(F32)
+        half[d] = total.astype(half.dtype)
+    copies = []
+    for k in range(1, depth):
+        peer = depth_peer(me, k, depth)
+        copies.append(
+            remote(
+                half.at[peer // PLANE],
+                got_depth.at[k - 1],
+                sems[2].at[k - 1],
+                sems[3].at[k - 1],
+                {"seq": peer},
+            )
+        )
+    wait_all(copies)
+    total = half[z].astype(F32)
+    for k in range(depth - 1):
+        total = total + got_depth[k].astype(F32)
+    return total
+
+
+def gather_rows(n, me, whole, sems):
+    depth = n // PLANE
+    z, p = me // PLANE, me % PLANE
+    wait_all(
+        [
+            remote(
+                whole.at[z, p],
+                whole.at[z, p],
+                sems[0].at[k - 1],
+                sems[1].at[k - 1],
+                {"seq": depth_peer(me, k, depth)},
+            )
+            for k in range(1, depth)
+        ]
+    )
+    wait_all(
+        [
+            remote(
+                whole.at[:, p],
+                whole.at[:, p],
+                sems[2].at[j - 1],
+                sems[3].at[j - 1],
+                {"seq": plane_peer(me, j)},
+            )
+            for j in range(1, PLANE)
+        ]
+    )
+
+
+def row_stats(n, me, widened, slots, send, recv):
+    rows = widened.shape[0]
+    lanes = lax.broadcasted_iota(jnp.int32, (rows, 128), 1)
+    first = jnp.sum(widened, axis=-1, keepdims=True)
+    second = jnp.sum(widened * widened, axis=-1, keepdims=True)
+    packed = jnp.where(lanes == 0, first, jnp.where(lanes == 1, second, 0.0))
+    slots[me] = packed.T[0:8]
+    share_small(n, me, slots, send, recv)
+    total = slots[0]
+    for i in range(1, n):
+        total = total + slots[i]
+    back = jnp.concatenate([total, jnp.zeros((120, rows), F32)], axis=0).T
+    return back[:, 0:1], back[:, 1:2]
+
+
+def normalize_rows(widened, first, second):
+    mean = first / D
+    inverse = 1.0 / jnp.sqrt(second / D - mean * mean + EPS)
+    return ((widened - mean) * inverse).astype(BF16)
+
+
+def project_kernel(
+    n, x_ref, wq, wk, wv, cos_ref, sin_ref, whole, own, part, got_plane, half, got_depth, slots, *sems
+):
+    me = lax.axis_index("seq")
+    enter(n, me)
+    widened = x_ref[...].astype(F32)
+    normed = normalize_rows(widened, *row_stats(n, me, widened, slots, sems[0], sems[1]))
+    width = wq.shape[1]
+    shape = part.shape[:3] + (width,)
+    for i, w in enumerate((wq, wk, wv)):
+        made = jnp.dot(normed, w[...], preferred_element_type=F32)
+        part[:, :, :, i * width : (i + 1) * width] = made.reshape(shape)
+    sums = scatter_sum(n, me, part, got_plane, half, got_depth, sems[2:6])
+    cosine, sine = cos_ref[me], sin_ref[me]
+    z, p = me // PLANE, me % PLANE
+    for c in range(3 * width // 128):
+        piece = sums[:, c * 128 : (c + 1) * 128]
+        if c < 2 * width // 128:
+            piece = piece * cosine + pltpu.roll(piece, 64, 1) * sine
+        whole[z, p, :, c * 128 : (c + 1) * 128] = piece.astype(BF16)
+    own[...] = whole[z, p]
+    gather_rows(n, me, whole, sems[6:10])
+
+
+def attend_kernel(
+    n,
+    scale,
+    stat_ref,
+    acc_ref,
+    own_ref,
+    x_ref,
+    w_ref,
+    mixed_ref,
+    normed_ref,
+    part,
+    got_plane,
+    half,
+    got_depth,
+    tops,
+    slots,
+    back_ref,
+    whole,
+    mine,
+    other,
+    *sems,
+):
+    me = lax.axis_index("seq")
+    partner = 1 - lax.axis_index("mdl")
+    enter(n, me, partner)
+    rows = stat_ref.shape[0]
+    width = acc_ref.shape[1]
+    heads = width // 128
+    stat = stat_ref[...]
+    tops[me] = stat.T[0:8]
+    share_small(n, me, tops, sems[0], sems[1])
+    top = tops[0]
+    for i in range(1, n):
+        top = jnp.maximum(top, tops[i])
+    back = jnp.concatenate([top, jnp.zeros((120, rows), F32)], axis=0).T
+    back_ref[...] = back.reshape(back_ref.shape)
+    factor = jnp.exp(stat - back)
+    shape = part.shape[:3] + (128,)
+    for h in range(heads):
+        cols = slice(h * 128, (h + 1) * 128)
+        part[:, :, :, cols] = (acc_ref[:, cols] * factor[:, h : h + 1]).reshape(shape)
+    lanes = lax.broadcasted_iota(jnp.int32, (rows, 128), 1)
+    totals = jnp.where(lanes < heads, pltpu.roll(stat, 128 - heads, 1) * factor, 0.0)
+    part[:, :, :, width : width + 128] = totals.reshape(shape)
+    sums = scatter_sum(n, me, part, got_plane, half, got_depth, sems[2:6])
+    z, p = me // PLANE, me % PLANE
+    top_own = back_ref[me]
+    token = lax.broadcasted_iota(jnp.int32, (8, 8), 0)
+    key = lax.broadcasted_iota(jnp.int32, (8, 8), 1)
+    allowed = (token // 4 == key // 4) & (key <= token)
+    for h in range(heads):
+        cols = slice(h * 128, (h + 1) * 128)
+        query = own_ref[:, h * 128 : (h + 1) * 128]
+        keys = own_ref[:, width + h * 128 : width + (h + 1) * 128]
+        values = own_ref[:, 2 * width + h * 128 : 2 * width + (h + 1) * 128]
+        scores = (
+            lax.dot_general(query, keys, (((1,), (1,)), ((), ())), preferred_element_type=F32)
+            * scale
+        )
+        scores = jnp.where(allowed, scores, NEGATIVE)
+        top_cache = top_own[:, h : h + 1]
+        top_all = jnp.maximum(top_cache, jnp.max(scores, axis=-1, keepdims=True))
+        weights = jnp.where(allowed, jnp.exp(scores - top_all), 0.0)
+        kept = jnp.exp(top_cache - top_all)
+        running = sums[:, width + h : width + h + 1] * kept + jnp.sum(
+            weights, axis=-1, keepdims=True
+        )
+        summed = sums[:, cols] * kept + jnp.dot(
+            weights,
+            values.astype(F32),
+            precision=lax.Precision.HIGHEST,
+            preferred_element_type=F32,
+        )
+        whole[z, p, :, cols] = (summed / running).astype(BF16)
+    gather_rows(n, me, whole, sems[6:10])
+    attended = whole[...].astype(F32).reshape(rows, width).astype(BF16)
+    made = jnp.dot(attended, w_ref[...], preferred_element_type=F32)
+    mine[...] = made
+    remote(mine, other, sems[12].at[0], sems[13].at[0], {"mdl": partner}).wait()
+    mixed = x_ref[...].astype(F32) + (made + other[...])
+    mixed_ref[...] = mixed
+    normed_ref[...] = normalize_rows(
+        mixed, *row_stats(n, me, mixed, slots, sems[10], sems[11])
+    )
+
+
+def feed_kernel(
+    n,
+    normed_ref,
+    mixed_ref,
+    wg,
+    wu,
+    wd,
+    out_ref,
+    part,
+    got_plane,
+    half,
+    got_depth,
+    whole,
+    mine,
+    other,
+    *sems,
+):
+    me = lax.axis_index("seq")
+    partner = 1 - lax.axis_index("mdl")
+    enter(n, me, partner)
+    rows = normed_ref.shape[0]
+    width = wg.shape[1]
+    tile = 1024
+    normed = normed_ref[...]
+    shape = part.shape[:3] + (tile,)
+    for i, w in enumerate((wg, wu)):
+        for t in range(0, width, tile):
+            made = jnp.dot(normed, w[:, t : t + tile], preferred_element_type=F32)
+            part[:, :, :, i * width + t : i * width + t + tile] = made.reshape(shape).astype(
+                part.dtype
+            )
+    sums = scatter_sum(n, me, part, got_plane, half, got_depth, sems[0:4])
+    z, p = me // PLANE, me % PLANE
+    gate, up = sums[:, :width], sums[:, width:]
+    whole[z, p] = (gate / (1.0 + jnp.exp(-gate)) * up).astype(BF16)
+    gather_rows(n, me, whole, sems[4:8])
+    total = jnp.zeros((rows, out_ref.shape[1]), F32)
+    for t in range(0, width, tile):
+        act = whole[:, :, :, t : t + tile].astype(F32).reshape(rows, tile).astype(BF16)
+        total = total + jnp.dot(act, wd[t : t + tile], preferred_element_type=F32)
+    mine[...] = total
+    remote(mine, other, sems[8].at[0], sems[9].at[0], {"mdl": partner}).wait()
+    out_ref[...] = mixed_ref[...] + (total + other[...])
+
+
+def pair(count):
+    return [pltpu.SemaphoreType.DMA((count,))] * 2
+
+
+def call(kernel, identity, outs, scratch, *operands):
+    vmem = pl.BlockSpec(memory_space=pltpu.VMEM)
+    return pl.pallas_call(
+        kernel,
+        out_shape=outs,
+        in_specs=[vmem] * len(operands),
+        out_specs=[vmem] * len(outs),
+        scratch_shapes=scratch,
+        compiler_params=pltpu.CompilerParams(
+            collective_id=identity, has_side_effects=True, vmem_limit_bytes=48 * 2**20
+        ),
+    )(*operands)
+
+
+def sum_scratch(depth, width, dtype):
+    return [
+        pltpu.VMEM((depth, PLANE, 8, width), dtype),
+        pltpu.VMEM((PLANE - 1, depth, 8, width), dtype),
+        pltpu.VMEM((depth, 8, width), dtype),
+        pltpu.VMEM((depth - 1, 8, width), dtype),
+    ]
+
+
+def body_kernels(
+    n,
+    hidden_in,
+    cache_keys,
+    cache_values,
+    lengths,
+    query_weight,
+    key_weight,
+    value_weight,
+    out_weight,
+    gate_weight,
+    up_weight,
+    down_weight,
+):
+    requests, token_count, narrow = hidden_in.shape
+    rows = requests * token_count
+    depth = n // PLANE
+    slot_count, local_width = cache_keys.shape[1:]
+    head_size = D // HEADS
+    local_heads = local_width // head_size
+    score_scale = 1.0 / math.sqrt(head_size)
+    shard_index = lax.axis_index("seq")
+    slot_ids = shard_index * slot_count + jnp.arange(slot_count, dtype=jnp.int32)
+    live_slots = slot_ids[None, :] < lengths[:, None]
+    positions = lengths[:, None] + jnp.arange(token_count, dtype=jnp.int32)[None, :]
+    half_dim = head_size // 2
+    freqs = THETA ** (-jnp.arange(half_dim, dtype=F32) * 2.0 / head_size)
+    angles = positions.reshape(rows, 1).astype(F32) * freqs
+    cosine, sine = jnp.cos(angles), jnp.sin(angles)
+    cosine = jnp.concatenate([cosine, cosine], axis=-1).reshape(n, 8, head_size)
+    sine = jnp.concatenate([-sine, sine], axis=-1).reshape(n, 8, head_size)
+    x = hidden_in.reshape(rows, narrow)
+    struct = jax.ShapeDtypeStruct
+    whole, own = call(
+        functools.partial(project_kernel, n),
+        1,
+        [struct((depth, PLANE, 8, 3 * local_width), BF16), struct((8, 3 * local_width), BF16)],
+        sum_scratch(depth, 3 * local_width, F32)
+        + [pltpu.VMEM((n, 8, 128), F32)]
+        + pair(n - 1)
+        + pair(PLANE - 1)
+        + pair(depth - 1)
+        + pair(depth - 1)
+        + pair(PLANE - 1),
+        x,
+        query_weight,
+        key_weight,
+        value_weight,
+        cosine,
+        sine,
+    )
+    whole = whole.reshape(requests, token_count, 3 * local_width)
+    keys_all = whole[..., local_width : 2 * local_width]
+    values_all = whole[..., 2 * local_width :]
+    queries = whole[..., :local_width].reshape(requests, token_count, local_heads, head_size)
+    old_keys = cache_keys.reshape(requests, slot_count, local_heads, head_size)
+    old_values = cache_values.reshape(requests, slot_count, local_heads, head_size).astype(F32)
+    old_scores = (
+        jnp.einsum("rnhd,rjhd->rnhj", queries, old_keys, preferred_element_type=F32) * score_scale
+    )
+    old_scores = jnp.where(live_slots[:, None, None, :], old_scores, NEGATIVE)
+    top_old = jnp.max(old_scores, axis=-1)
+    weights_old = jnp.where(
+        live_slots[:, None, None, :], jnp.exp(old_scores - top_old[..., None]), 0.0
+    )
+    total_old = jnp.sum(weights_old, axis=-1)
+    summed_old = jnp.einsum(
+        "rnhj,rjhd->rnhd", weights_old, old_values, precision=lax.Precision.HIGHEST
+    )
+    stat = jnp.concatenate(
+        [
+            top_old.reshape(rows, local_heads),
+            total_old.reshape(rows, local_heads),
+            jnp.zeros((rows, 128 - 2 * local_heads), F32),
+        ],
+        axis=-1,
+    )
+    mixed, normed2 = call(
+        functools.partial(attend_kernel, n, score_scale),
+        2,
+        [struct((rows, narrow), F32), struct((rows, narrow), BF16)],
+        sum_scratch(depth, local_width + 128, F32)
+        + [
+            pltpu.VMEM((n, 8, 128), F32),
+            pltpu.VMEM((n, 8, 128), F32),
+            pltpu.VMEM((n, 8, 128), F32),
+            pltpu.VMEM((depth, PLANE, 8, local_width), BF16),
+            pltpu.VMEM((rows, narrow), F32),
+            pltpu.VMEM((rows, narrow), F32),
+        ]
+        + pair(n - 1)
+        + pair(PLANE - 1)
+        + pair(depth - 1)
+        + pair(depth - 1)
+        + pair(PLANE - 1)
+        + pair(n - 1)
+        + pair(1),
+        stat,
+        summed_old.reshape(rows, local_width),
+        own,
+        x,
+        out_weight,
+    )
+    ff = gate_weight.shape[1]
+    (block_out,) = call(
+        functools.partial(feed_kernel, n),
+        3,
+        [struct((rows, narrow), F32)],
+        sum_scratch(depth, 2 * ff, BF16)
+        + [
+            pltpu.VMEM((depth, PLANE, 8, ff), BF16),
+            pltpu.VMEM((rows, narrow), F32),
+            pltpu.VMEM((rows, narrow), F32),
+        ]
+        + pair(PLANE - 1)
+        + pair(depth - 1)
+        + pair(depth - 1)
+        + pair(PLANE - 1)
+        + pair(1),
+        normed2,
+        mixed,
+        gate_weight,
+        up_weight,
+        down_weight,
+    )
+    hidden_out = block_out.astype(BF16).reshape(requests, token_count, narrow)
+    new_keys, new_values = write_rows(
+        slot_ids, positions, keys_all, values_all, cache_keys, cache_values
+    )
+    return hidden_out, new_keys, new_values
+
+
+def write_rows(slot_ids, positions, keys_all, values_all, cache_keys, cache_values):
+    slot_hits = slot_ids[None, None, :] == positions[:, :, None]
+    one_hot = slot_hits.astype(BF16)
+    written = jnp.any(slot_hits, axis=1)[..., None]
+    placed = [
+        jnp.einsum("rts,rtm->rsm", one_hot, rows, preferred_element_type=F32).astype(BF16)
+        for rows in (keys_all, values_all)
+    ]
+    return (
+        jnp.where(written, placed[0], cache_keys),
+        jnp.where(written, placed[1], cache_values),
+    )
+
+
+def body(n, model_shards, hidden_in, cache_keys, *rest):
+    rows = hidden_in.shape[0] * hidden_in.shape[1]
+    tiled = (
+        n % PLANE == 0
+        and rows == 128
+        and rows // n == 8
+        and hidden_in.shape[1] == 4
+        and hidden_in.shape[2] == 128
+        and model_shards == 2
+    )
+    if tiled:
+        return body_kernels(n, hidden_in, cache_keys, *rest)
+    return body_plain(hidden_in, cache_keys, *rest)
+
+
 def solution(mesh):
     placed = (
         P(None, None, "seq"),
@@ -199,7 +690,7 @@
         P("mdl", "seq"),
     )
     return jax.shard_map(
-        body,
+        functools.partial(body, mesh.shape["seq"], mesh.shape["mdl"]),
         mesh=mesh,
         in_specs=placed,
         out_specs=(P(None, None, "seq"), P(None, "seq", "mdl"), P(None, "seq", "mdl")),

time: 623 us -> 176 us (0.28)
  waiting for transfers between devices: 319 us -> 0 us
  blocking collectives: 243 us -> 0 us
  Pallas kernels: 0 us -> 146 us
  matrix products: 31 us -> 12.9 us
  between operations: 14.1 us -> 0.82 us
    psum x5 -> x0, waiting for transfers between devices: 319 us -> none  [the longest x1 160 us: body(): gate_full, up_full = lax.psum((gate_part, up_part), 'seq')]
    psum x3 -> x0, blocking collectives: 167 us -> none  [the longest x1 82 us: body(): lax.psum((query_part, key_part, value_part), 'seq')]
    pallas_call x0 -> x3, Pallas kernels: none -> 146 us  [call(): pl.pallas_call(kernel, out_shape=outs, in_specs=[vmem] * len(operands), o...]
    pmax x1 -> x0, blocking collectives: 75.7 us -> none  [body(): top_cache = lax.pmax(top_old, 'seq')]
    dot_general x13 -> x4, matrix products: 31 us -> 12.9 us  [the longest x2 5.32 us: write_rows(): jnp.einsum('rts,rtm->rsm', one_hot, rows, preferred_element_type=F32)]
  transfers between devices with their start and end apart: 5 -> 0, of which waited for: 5 -> 0; matrix products, arithmetic and copies ran while one was open for 2% -> 0% of each run, Pallas kernels for 0% -> 0%
where the time goes in v2:
time: 176 us
  Pallas kernels  146 us (83%)
  matrix products  12.9 us (7%)
  local copies, waits for them, and re-layouts  10.1 us (6%)
  other arithmetic  5.82 us (3%)
    pallas_call x3, Pallas kernels, call(): pl.pallas_call(kernel, out_shape=outs, in_specs=[vmem] * len(operands), o...  146 us
    dot_general x2, matrix products, write_rows(): jnp.einsum('rts,rtm->rsm', one_hot, rows, preferred_element_type=F32)  5.32 us
    dot_general x1, matrix products, body_kernels(): jnp.einsum('rnhd,rjhd->rnhj', queries, old_keys, preferred_element_type=F32)  3.83 us
    unnamed x31, local copies, waits for them, and re-layouts  3.75 us
    dot_general x1, matrix products, body_kernels(): jnp.einsum('rnhj,rjhd->rnhd', weights_old, old_values, precision=lax.Prec...  3.73 us

profile of v2, /device:TPU:0, one launch (start us, length us, event | category | flops | bytes accessed | tf_op | source)
XLA Modules:
  0.0 176.0 jit_solution(4778448813304241550)
XLA Ops:
  0.7 0.1 pad.2.clone
  0.7 0.7 broadcast_compare_fusion
  1.5 0.7 add.50
  2.2 0.1 copy.28
  2.3 0.7 iota_add_fusion
  3.0 0.1 compare_reduce_fusion
  3.2 0.1 add.54
  3.2 0.1 copy.29
  3.3 0.1 copy.30
  3.4 0.3 fusion.30
  3.7 0.1 pad_maximum_fusion
  3.8 0.0 copy-start.4
  3.8 0.9 copy-done.4
  4.8 0.0 copy-start.5
  4.8 0.9 copy-done.5
  5.7 0.0 copy-start.6
  5.7 0.9 copy-done.6
  6.7 0.0 copy-start.7
  6.7 0.8 copy-done.7
  7.4 50.8 %shard_map.130 = (bf16[4,4,8,3072]{3,2,1,0:T(8,128)(2,1)S(1)}, bf16[8,3072]{1,0:T(8,128)(2,1)S(1)}) custom-call(bf16[128,128]{1,0:T(8,128)(2,1)S(1)} %bitcast.46, bf16[128,1024]{1,0:T(8,128)(2,1)S(1)} %copy-done.4, bf16[128,1024]{1,0:T(8,128)(2,1)S(1)} %copy-done.5, bf16[128,1024]{1,0:T(8,128)(2,1)S(1)} %copy-done.6, ...), custom_call_target="tpu_custom_call" | custom-call | tf_op jit(solution)/shard_map/pallas_call | solution.py:496
  58.2 0.3 reshape.155
  58.5 0.0 copy-start.9
  58.5 0.0 copy-start.11
  58.5 3.8 %fusion.32 = (f32[32,4,8]{1,2,0:T(8,128)}, f32[32,4,8,32]{3,1,2,0:T(4,128)S(1)}) fusion(bf16[32,4,3072]{2,1,0:T(4,128)(2,1)S(1)} %reshape.155, pred[32,32]{1,0:T(8,128)(4,1)S(1)} %broadcast_compare_fusion, bf16[32,32,1024]{2,1,0:T(8,128)(2,1)} %param.12), kind=kOutput, calls=%fused_computation.40 | convolution fusion | flops 8485888 | bytes 2498560 | tf_op jit(solution)/shard_map/rnhd,rjhd->rnhj/dot_general | solution.py:575
  62.4 0.0 copy-start.14
  62.4 1.9 %copy.32 = f32[32,4,8]{2,1,0:T(4,128)} copy(f32[32,4,8]{1,2,0:T(8,128)} %get-tuple-element.14) | data formatting | bytes 8192 | tf_op jit(solution)/shard_map/reduce_max | solution.py:578
  64.3 0.0 copy-done.14
  64.3 2.2 %fusion.18 = f32[32,4,8]{1,2,0:T(8,128)} fusion(f32[32,4,8,32]{3,1,2,0:T(4,128)S(1)} %get-tuple-element.15, f32[32,4,8]{1,2,0:T(8,128)} %get-tuple-element.14, pred[32,32]{1,0:T(8,128)(4,1)S(1)} %broadcast_compare_fusion), kind=kLoop, calls=%fused_computation.14 | loop fusion | flops 97280 | bytes 140288 | tf_op jit(solution)/shard_map/reduce_sum | solution.py:582
  66.5 0.0 copy-done.9
  66.5 0.0 copy-done.11
  66.5 0.0 copy-start.3
  66.5 0.0 copy-start.8
  66.5 3.7 %fusion.6 = f32[32,4,8,128]{3,1,2,0:T(4,128)} fusion(f32[32,4,8,32]{3,1,2,0:T(4,128)} %copy-done.14, f32[32,4,8]{1,2,0:T(8,128)} %get-tuple-element.14, pred[32,32]{1,0:T(8,128)(4,1)S(1)} %broadcast_compare_fusion, bf16[32,32,1024]{2,1,0:T(8,128)(2,1)S(1)} %copy-done.11), kind=kOutput, calls=%fused_computation.8 | convolution fusion | flops 50397184 | bytes 2757632 | tf_op jit(solution)/shard_map/rnhj,rjhd->rnhd/dot_general | solution.py:583
  70.2 0.0 copy-start
  70.2 0.0 copy-start.1
  70.2 0.0 copy-start.2
  70.3 1.9 %copy.33 = f32[32,4,8]{2,1,0:T(4,128)} copy(f32[32,4,8]{1,2,0:T(8,128)} %fusion.18) | data formatting | bytes 8192 | tf_op jit(solution)/shard_map/reduce_sum | solution.py:582
  72.2 1.0 maximum_maximum_fusion.stat_ref
  73.2 1.1 copy.35
  74.2 0.1 copy.58
  74.3 0.0 copy-done.3
  74.3 0.0 copy-done.8
  74.4 0.0 copy-start.10
  74.4 0.0 copy-start.12
  74.4 38.0 %shard_map.131 = (f32[128,128]{1,0:T(8,128)S(1)}, bf16[128,128]{1,0:T(8,128)(2,1)S(1)}) custom-call(f32[128,128]{1,0:T(8,128)S(1)} %maximum_maximum_fusion.stat_ref, f32[128,1024]{1,0:T(8,128)S(1)} %bitcast.45, bf16[8,3072]{1,0:T(8,128)(2,1)S(1)} %get-tuple-element.8.own_ref, bf16[128,128]{1,0:T(8,128)(2,1)S(1)} %bitcast.47, bf16[1024,128]{1,0:T(8,128)(2,1)S(1)} %copy-done.3), custom_call_target="tpu_custom_call" | custom-call | tf_op jit(solution)/shard_map/pallas_call | solution.py:496
  112.4 0.0 copy-done
  112.4 0.0 copy-done.1
  112.4 0.0 copy-done.2
  112.4 57.6 %shard_map.132 = f32[128,128]{1,0:T(8,128)S(1)} custom-call(bf16[128,128]{1,0:T(8,128)(2,1)S(1)} %get-tuple-element.9.normed_ref, f32[128,128]{1,0:T(8,128)S(1)} %get-tuple-element.10.mixed_ref, bf16[128,4096]{1,0:T(8,128)(2,1)S(1)} %copy-done, bf16[128,4096]{1,0:T(8,128)(2,1)S(1)} %copy-done.1, bf16[4096,128]{1,0:T(8,128)(2,1)S(1)} %copy-done.2), custom_call_target="tpu_custom_call" | custom-call | tf_op jit(solution)/shard_map/pallas_call | solution.py:496
  170.0 0.6 convert_element_type.20
  170.7 0.0 copy-done.10
  170.7 0.0 copy-done.12
  170.7 0.0 copy-start.13
  170.7 2.6 %convert_select_fusion = bf16[32,32,1024]{2,1,0:T(8,128)(2,1)} fusion(bf16[32,32,1024]{2,1,0:T(8,128)(2,1)S(1)} %copy-done.12, pred[32,32]{1,0:T(8,128)(4,1)S(1)} %compare_reduce_fusion, bf16[32,4,3072]{2,1,0:T(4,128)(2,1)S(1)} %copy-done.10, s32[32,4]{1,0:T(8,128)S(1)} %iota_add_fusion, s32[32]{0:T(128)S(1)} %iota_add_fusion.1), kind=kOutput, calls=%fused_computation.6 | convolution fusion | flops 10489856 | bytes 4477440 | tf_op jit(solution)/shard_map/rts,rtm->rsm/dot_general | solution.py:654
  173.3 0.0 copy-done.13
  173.3 2.7 %convert_select_fusion.1 = bf16[32,32,1024]{2,1,0:T(8,128)(2,1)} fusion(bf16[32,32,1024]{2,1,0:T(8,128)(2,1)S(1)} %copy-done.13, pred[32,32]{1,0:T(8,128)(4,1)S(1)} %compare_reduce_fusion, bf16[32,4,3072]{2,1,0:T(4,128)(2,1)S(1)} %copy-done.10, s32[32,4]{1,0:T(8,128)S(1)} %iota_add_fusion, s32[32]{0:T(128)S(1)} %iota_add_fusion.1), kind=kOutput, calls=%fused_computation.7 | convolution fusion | flops 10489856 | bytes 4477440 | tf_op jit(solution)/shard_map/rts,rtm->rsm/dot_general | solution.py:654
  (6 shorter events, 0.0 us)
Async XLA Ops:
  3.8 1.0 copy-start.4
  4.8 0.9 copy-start.5
  5.7 0.9 copy-start.6
  6.7 0.8 copy-start.7
  58.5 8.0 %copy-start.9 = (bf16[32,4,3072]{2,1,0:T(4,128)(2,1)}, bf16[32,4,3072]{2,1,0:T(4,128)(2,1)S(1)}, u32[]{:S(2)}) copy-start(bf16[32,4,3072]{2,1,0:T(4,128)(2,1)S(1)} %reshape.155) | copy-start | bytes 2359300
  58.5 8.0 %copy-start.11 = (bf16[32,32,1024]{2,1,0:T(8,128)(2,1)S(1)}, bf16[32,32,1024]{2,1,0:T(8,128)(2,1)}, u32[]{:S(2)}) copy-start(bf16[32,32,1024]{2,1,0:T(8,128)(2,1)} %param.13) | copy-start | bytes 6291460
  62.4 1.9 %copy-start.14 = (f32[32,4,8,32]{3,1,2,0:T(4,128)}, f32[32,4,8,32]{3,1,2,0:T(4,128)S(1)}, u32[]{:S(2)}) copy-start(f32[32,4,8,32]{3,1,2,0:T(4,128)S(1)} %get-tuple-element.15) | copy-start | bytes 393220
  66.5 7.8 %copy-start.3 = (bf16[1024,128]{1,0:T(8,128)(2,1)S(1)}, bf16[1024,128]{1,0:T(8,128)(2,1)}, u32[]{:S(2)}) copy-start(bf16[1024,128]{1,0:T(8,128)(2,1)} %w_ref.1) | copy-start | bytes 786436
  66.5 7.8 %copy-start.8 = (bf16[32,4,128]{2,1,0:T(4,128)(2,1)S(1)}, bf16[32,4,128]{2,1,0:T(4,128)(2,1)}, u32[]{:S(2)}) copy-start(bf16[32,4,128]{2,1,0:T(4,128)(2,1)} %param.11) | copy-start | bytes 98308
  70.2 42.2 %copy-start = (bf16[128,4096]{1,0:T(8,128)(2,1)S(1)}, bf16[128,4096]{1,0:T(8,128)(2,1)}, u32[]{:S(2)}) copy-start(bf16[128,4096]{1,0:T(8,128)(2,1)} %wg.1) | copy-start | bytes 3145732
  70.2 42.2 %copy-start.1 = (bf16[128,4096]{1,0:T(8,128)(2,1)S(1)}, bf16[128,4096]{1,0:T(8,128)(2,1)}, u32[]{:S(2)}) copy-start(bf16[128,4096]{1,0:T(8,128)(2,1)} %wu.1) | copy-start | bytes 3145732
  70.2 42.2 %copy-start.2 = (bf16[4096,128]{1,0:T(8,128)(2,1)S(1)}, bf16[4096,128]{1,0:T(8,128)(2,1)}, u32[]{:S(2)}) copy-start(bf16[4096,128]{1,0:T(8,128)(2,1)} %wd.1) | copy-start | bytes 3145732
  74.4 96.3 %copy-start.10 = (bf16[32,4,3072]{2,1,0:T(4,128)(2,1)S(1)}, bf16[32,4,3072]{2,1,0:T(4,128)(2,1)}, u32[]{:S(2)}) copy-start(bf16[32,4,3072]{2,1,0:T(4,128)(2,1)} %copy-done.9) | copy-start | bytes 2359300
  74.4 96.3 %copy-start.12 = (bf16[32,32,1024]{2,1,0:T(8,128)(2,1)S(1)}, bf16[32,32,1024]{2,1,0:T(8,128)(2,1)}, u32[]{:S(2)}) copy-start(bf16[32,32,1024]{2,1,0:T(8,128)(2,1)} %param.13) | copy-start | bytes 6291460
  170.7 2.6 %copy-start.13 = (bf16[32,32,1024]{2,1,0:T(8,128)(2,1)S(1)}, bf16[32,32,1024]{2,1,0:T(8,128)(2,1)}, u32[]{:S(2)}) copy-start(bf16[32,32,1024]{2,1,0:T(8,128)(2,1)} %param.12) | copy-start | bytes 6291460

commit v3 on v1

--- a/solution.py
+++ b/solution.py
@@ -1,8 +1,11 @@
+import functools
 import math
 
 import jax
 import jax.numpy as jnp
 from jax import lax
+from jax.experimental import pallas as pl
+from jax.experimental.pallas import tpu as pltpu
 from jax.sharding import PartitionSpec as P
 
 D = 2048
@@ -36,7 +39,7 @@
     return ((widened - row_mean[..., None]) * inverse[..., None]).astype(jnp.bfloat16)
 
 
-def body(
+def body_plain(
     hidden_in,
     cache_keys,
     cache_values,
@@ -184,6 +187,550 @@
     return (hidden_out, new_cache_keys, new_cache_values)
 
 
+PLANE = 4
+MESH = pl.DeviceIdType.MESH
+F32 = jnp.float32
+BF16 = jnp.bfloat16
+
+
+def plane_peer(me, j):
+    p = me % PLANE
+    x, y = p % 2, p // 2
+    if j % 2:
+        x = 1 - x
+    if j // 2:
+        y = 1 - y
+    return (me // PLANE) * PLANE + y * 2 + x
+
+
+def depth_peer(me, k, depth):
+    return ((me // PLANE + k) % depth) * PLANE + me % PLANE
+
+
+def remote(src, dst, send, recv, device):
+    copy = pltpu.make_async_remote_copy(
+        src_ref=src, dst_ref=dst, send_sem=send, recv_sem=recv, device_id=device, device_id_type=MESH
+    )
+    copy.start()
+    return copy
+
+
+def wait_all(copies):
+    for copy in copies:
+        copy.wait()
+
+
+def enter(n, me, partner=None):
+    barrier = pltpu.get_barrier_semaphore()
+    for k in range(1, n):
+        pl.semaphore_signal(
+            barrier, inc=1, device_id={"seq": (me + k) % n}, device_id_type=MESH
+        )
+    if partner is not None:
+        pl.semaphore_signal(barrier, inc=1, device_id={"mdl": partner}, device_id_type=MESH)
+    pl.semaphore_wait(barrier, n - 1 + (partner is not None))
+
+
+def share_small(n, me, slots, send, recv):
+    wait_all(
+        [
+            remote(
+                slots.at[me], slots.at[me], send.at[k - 1], recv.at[k - 1], {"seq": (me + k) % n}
+            )
+            for k in range(1, n)
+        ]
+    )
+
+
+def pipeline(
+    n, me, fill, finish, consume, part, got_plane, half, got_depth, whole, *sems
+):
+    depth = n // PLANE
+    chunks = part.shape[0]
+    z, p = me // PLANE, me % PLANE
+    flying = {}
+
+    def send(kind, c, src, dst, pair_at, device):
+        flying.setdefault((kind, c), []).append(
+            remote(src, dst, sems[2 * kind].at[pair_at], sems[2 * kind + 1].at[pair_at], {"seq": device})
+        )
+
+    for c in range(chunks):
+        fill(c)
+        for j in range(1, PLANE):
+            peer = plane_peer(me, j)
+            send(
+                0,
+                c,
+                part.at[c, :, peer % PLANE],
+                got_plane.at[c, j - 1],
+                c * (PLANE - 1) + j - 1,
+                peer,
+            )
+    for step in range(chunks + 3):
+        c = step
+        if c < chunks:
+            wait_all(flying[0, c])
+            for d in range(depth):
+                total = part[c, d, p].astype(F32)
+                for j in range(PLANE - 1):
+                    total = total + got_plane[c, j, d].astype(F32)
+                half[c, d] = total.astype(half.dtype)
+            for k in range(1, depth):
+                peer = depth_peer(me, k, depth)
+                send(
+                    1,
+                    c,
+                    half.at[c, peer // PLANE],
+                    got_depth.at[c, k - 1],
+                    c * (depth - 1) + k - 1,
+                    peer,
+                )
+        c = step - 1
+        if 0 <= c < chunks:
+            wait_all(flying[1, c])
+            total = half[c, z].astype(F32)
+            for k in range(depth - 1):
+                total = total + got_depth[c, k].astype(F32)
+            finish(c, total)
+            for k in range(1, depth):
+                mine = whole.at[c, z, p]
+                send(
+                    2, c, mine, mine, c * (depth - 1) + k - 1, depth_peer(me, k, depth)
+                )
+        c = step - 2
+        if 0 <= c < chunks:
+            wait_all(flying[2, c])
+            for j in range(1, PLANE):
+                mine = whole.at[c, :, p]
+                send(3, c, mine, mine, c * (PLANE - 1) + j - 1, plane_peer(me, j))
+        c = step - 3
+        if 0 <= c < chunks:
+            wait_all(flying[3, c])
+            consume(c)
+
+
+def row_stats(n, me, widened, slots, send, recv):
+    rows = widened.shape[0]
+    lanes = lax.broadcasted_iota(jnp.int32, (rows, 128), 1)
+    first = jnp.sum(widened, axis=-1, keepdims=True)
+    second = jnp.sum(widened * widened, axis=-1, keepdims=True)
+    packed = jnp.where(lanes == 0, first, jnp.where(lanes == 1, second, 0.0))
+    slots[me] = packed.T[0:8]
+    share_small(n, me, slots, send, recv)
+    total = slots[0]
+    for i in range(1, n):
+        total = total + slots[i]
+    back = jnp.concatenate([total, jnp.zeros((120, rows), F32)], axis=0).T
+    return back[:, 0:1], back[:, 1:2]
+
+
+def normalize_rows(widened, first, second):
+    mean = first / D
+    inverse = 1.0 / jnp.sqrt(second / D - mean * mean + EPS)
+    return ((widened - mean) * inverse).astype(BF16)
+
+
+def project_kernel(
+    n, x_ref, wq, wk, wv, cos_ref, sin_ref, whole, own, held, arrived, slots, send, recv, *rest
+):
+    me = lax.axis_index("seq")
+    loads = [
+        pltpu.make_async_copy(w, held.at[i], arrived.at[i]) for i, w in enumerate((wq, wk, wv))
+    ]
+    for load in loads:
+        load.start()
+    enter(n, me)
+    part, got_plane, half, got_depth = rest[:4]
+    widened = x_ref[...].astype(F32)
+    normed = normalize_rows(widened, *row_stats(n, me, widened, slots, send, recv))
+    z, p = me // PLANE, me % PLANE
+
+    def fill(c):
+        loads[c].wait()
+        made = jnp.dot(normed, held[c], preferred_element_type=F32)
+        part[c] = made.reshape(part.shape[1:])
+
+    def finish(c, sums):
+        for i in range(sums.shape[1] // 128):
+            piece = sums[:, i * 128 : (i + 1) * 128]
+            if c < 2:
+                piece = piece * cos_ref[me] + pltpu.roll(piece, 64, 1) * sin_ref[me]
+            piece = piece.astype(BF16)
+            whole[c, z, p, :, i * 128 : (i + 1) * 128] = piece
+            own[c, :, i * 128 : (i + 1) * 128] = piece
+
+    pipeline(
+        n, me, fill, finish, lambda c: None, part, got_plane, half, got_depth, whole, *rest[4:]
+    )
+
+
+def cache_kernel(scale, len_ref, new_ref, k_ref, v_ref, stat_ref, acc_ref, ko_ref, vo_ref):
+    step = pl.program_id(0)
+    group, slots, width = k_ref.shape
+    base = lax.axis_index("seq") * slots
+    head_mask = lax.broadcasted_iota(jnp.int32, (8, width), 1) // 128 == (
+        lax.broadcasted_iota(jnp.int32, (8, width), 0)
+    )
+    slot = base + lax.broadcasted_iota(jnp.int32, (32, slots), 1)
+    sub = lax.broadcasted_iota(jnp.int32, (8, 128), 0)
+    lane = lax.broadcasted_iota(jnp.int32, (8, 128), 1)
+    for i in range(group):
+        length = len_ref[step * group + i]
+        at = (i % 2) * 4
+        fresh = [new_ref[c, i // 2].astype(F32) for c in range(3)]
+        keys, values = k_ref[i], v_ref[i]
+        queries = jnp.concatenate(
+            [jnp.where(head_mask, fresh[0][at + t : at + t + 1], 0.0) for t in range(4)], axis=0
+        ).astype(BF16)
+        scores = (
+            lax.dot_general(queries, keys, (((1,), (1,)), ((), ())), preferred_element_type=F32)
+            * scale
+        )
+        live = slot < length
+        scores = jnp.where(live, scores, NEGATIVE)
+        top = jnp.max(scores, axis=-1, keepdims=True)
+        weights = jnp.where(live, jnp.exp(scores - top), 0.0)
+        total = jnp.sum(weights, axis=-1, keepdims=True)
+        coarse = weights.astype(BF16)
+        fine = (weights - coarse.astype(F32)).astype(BF16)
+        summed = jnp.dot(coarse, values, preferred_element_type=F32) + jnp.dot(
+            fine, values, preferred_element_type=F32
+        )
+        for t in range(4):
+            row = i * 4 + t
+            part = slice(8 * t, 8 * t + 8)
+            acc_ref[row : row + 1] = jnp.sum(
+                jnp.where(head_mask, summed[part], 0.0), axis=0, keepdims=True
+            )
+            stat_ref[row : row + 1] = jnp.sum(
+                jnp.where(
+                    lane == sub, top[part], jnp.where(lane == sub + 8, total[part], 0.0)
+                ),
+                axis=0,
+                keepdims=True,
+            )
+        ko_ref[i] = keys
+        vo_ref[i] = values
+        first = length - base
+
+        @pl.when((first < slots) & (first > -4))
+        def _():
+            place = lax.broadcasted_iota(jnp.int32, (slots, width), 0)
+            for rows, old, out in ((fresh[1], keys, ko_ref), (fresh[2], values, vo_ref)):
+                held = old.astype(F32)
+                for t in range(4):
+                    held = jnp.where(place == first + t, rows[at + t : at + t + 1], held)
+                out[i] = held.astype(BF16)
+
+
+def attend_kernel(
+    n,
+    scale,
+    stat_ref,
+    acc_ref,
+    own_ref,
+    x_ref,
+    w_ref,
+    mixed_ref,
+    normed_ref,
+    tops,
+    slots,
+    back_ref,
+    mine,
+    other,
+    top_send,
+    top_recv,
+    send,
+    recv,
+    swap_send,
+    swap_recv,
+    *rest,
+):
+    me = lax.axis_index("seq")
+    partner = 1 - lax.axis_index("mdl")
+    enter(n, me, partner)
+    part, got_plane, half, got_depth, whole = rest[:5]
+    rows = stat_ref.shape[0]
+    heads = acc_ref.shape[1] // 128
+    chunks = part.shape[0]
+    each = heads // chunks
+    stat = stat_ref[...]
+    tops[me] = stat.T[0:8]
+    share_small(n, me, tops, top_send, top_recv)
+    top = tops[0]
+    for i in range(1, n):
+        top = jnp.maximum(top, tops[i])
+    back = jnp.concatenate([top, jnp.zeros((120, rows), F32)], axis=0).T
+    back_ref[...] = back.reshape(back_ref.shape)
+    factor = jnp.exp(stat - back)
+    shape = part.shape[1:4] + (128,)
+    lanes = lax.broadcasted_iota(jnp.int32, (rows, 128), 1)
+    totals = jnp.where(lanes < heads, pltpu.roll(stat, 128 - heads, 1) * factor, 0.0)
+    z, p = me // PLANE, me % PLANE
+    top_own = back_ref[me]
+    token = lax.broadcasted_iota(jnp.int32, (8, 8), 0)
+    key = lax.broadcasted_iota(jnp.int32, (8, 8), 1)
+    allowed = (token // 4 == key // 4) & (key <= token)
+
+    def fill(c):
+        for i in range(each):
+            h = c * each + i
+            part[c, :, :, :, i * 128 : (i + 1) * 128] = (
+                acc_ref[:, h * 128 : (h + 1) * 128] * factor[:, h : h + 1]
+            ).reshape(shape)
+        part[c, :, :, :, each * 128 :] = totals.reshape(shape)
+
+    def finish(c, sums):
+        for i in range(each):
+            h = c * each + i
+            cols = slice(h * 128, (h + 1) * 128)
+            query, keys, values = own_ref[0, :, cols], own_ref[1, :, cols], own_ref[2, :, cols]
+            scores = (
+                lax.dot_general(query, keys, (((1,), (1,)), ((), ())), preferred_element_type=F32)
+                * scale
+            )
+            scores = jnp.where(allowed, scores, NEGATIVE)
+            top_cache = top_own[:, h : h + 1]
+            top_all = jnp.maximum(top_cache, jnp.max(scores, axis=-1, keepdims=True))
+            weights = jnp.where(allowed, jnp.exp(scores - top_all), 0.0)
+            kept = jnp.exp(top_cache - top_all)
+            at = each * 128 + h
+            running = sums[:, at : at + 1] * kept + jnp.sum(weights, axis=-1, keepdims=True)
+            summed = sums[:, i * 128 : (i + 1) * 128] * kept + jnp.dot(
+                weights,
+                values.astype(F32),
+                precision=lax.Precision.HIGHEST,
+                preferred_element_type=F32,
+            )
+            whole[c, z, p, :, i * 128 : (i + 1) * 128] = (summed / running).astype(BF16)
+
+    def consume(c):
+        width = each * 128
+        attended = whole[c].astype(F32).reshape(rows, width).astype(BF16)
+        made = jnp.dot(
+            attended, w_ref[c * width : (c + 1) * width], preferred_element_type=F32
+        )
+        mine[...] = made if c == 0 else mine[...] + made
+
+    pipeline(n, me, fill, finish, consume, *rest)
+    remote(mine, other, swap_send.at[0], swap_recv.at[0], {"mdl": partner}).wait()
+    mixed = x_ref[...].astype(F32) + (mine[...] + other[...])
+    mixed_ref[...] = mixed
+    normed_ref[...] = normalize_rows(mixed, *row_stats(n, me, mixed, slots, send, recv))
+
+
+def feed_kernel(
+    n,
+    normed_ref,
+    mixed_ref,
+    wg,
+    wu,
+    wd,
+    out_ref,
+    mine,
+    other,
+    swap_send,
+    swap_recv,
+    *rest,
+):
+    me = lax.axis_index("seq")
+    partner = 1 - lax.axis_index("mdl")
+    enter(n, me, partner)
+    part, got_plane, half, got_depth, whole = rest[:5]
+    rows = normed_ref.shape[0]
+    tile = whole.shape[-1]
+    normed = normed_ref[...]
+    shape = part.shape[1:4] + (tile,)
+    z, p = me // PLANE, me % PLANE
+
+    def fill(c):
+        for i, w in enumerate((wg, wu)):
+            made = jnp.dot(
+                normed, w[:, c * tile : (c + 1) * tile], preferred_element_type=F32
+            )
+            part[c, :, :, :, i * tile : (i + 1) * tile] = made.reshape(shape).astype(part.dtype)
+
+    def finish(c, sums):
+        gate, up = sums[:, :tile], sums[:, tile:]
+        whole[c, z, p] = (gate / (1.0 + jnp.exp(-gate)) * up).astype(BF16)
+
+    def consume(c):
+        act = whole[c].astype(F32).reshape(rows, tile).astype(BF16)
+        made = jnp.dot(act, wd[c * tile : (c + 1) * tile], preferred_element_type=F32)
+        mine[...] = made if c == 0 else mine[...] + made
+
+    pipeline(n, me, fill, finish, consume, *rest)
+    remote(mine, other, swap_send.at[0], swap_recv.at[0], {"mdl": partner}).wait()
+    out_ref[...] = (mixed_ref[...] + (mine[...] + other[...])).astype(BF16)
+
+
+def pair(count):
+    return [pltpu.SemaphoreType.DMA((count,))] * 2
+
+
+def call(kernel, identity, outs, scratch, *operands, far=()):
+    vmem = pl.BlockSpec(memory_space=pltpu.VMEM)
+    return pl.pallas_call(
+        kernel,
+        out_shape=outs,
+        in_specs=[
+            pl.BlockSpec(memory_space=pl.ANY) if i in far else vmem for i in range(len(operands))
+        ],
+        out_specs=[vmem] * len(outs),
+        scratch_shapes=scratch,
+        compiler_params=pltpu.CompilerParams(
+            collective_id=identity, has_side_effects=True, vmem_limit_bytes=48 * 2**20
+        ),
+    )(*operands)
+
+
+def sum_scratch(chunks, depth, width, dtype):
+    return [
+        pltpu.VMEM((chunks, depth, PLANE, 8, width), dtype),
+        pltpu.VMEM((chunks, PLANE - 1, depth, 8, width), dtype),
+        pltpu.VMEM((chunks, depth, 8, width), dtype),
+        pltpu.VMEM((chunks, depth - 1, 8, width), dtype),
+    ]
+
+
+def pipe_sems(chunks, depth):
+    plane, line = pair(chunks * (PLANE - 1)), pair(chunks * (depth - 1))
+    return plane + line + line + plane
+
+
+def body_kernels(
+    n,
+    hidden_in,
+    cache_keys,
+    cache_values,
+    lengths,
+    query_weight,
+    key_weight,
+    value_weight,
+    out_weight,
+    gate_weight,
+    up_weight,
+    down_weight,
+):
+    requests, token_count, narrow = hidden_in.shape
+    rows = requests * token_count
+    depth = n // PLANE
+    slot_count, local_width = cache_keys.shape[1:]
+    head_size = D // HEADS
+    score_scale = 1.0 / math.sqrt(head_size)
+    positions = lengths[:, None] + jnp.arange(token_count, dtype=jnp.int32)[None, :]
+    half_dim = head_size // 2
+    freqs = THETA ** (-jnp.arange(half_dim, dtype=F32) * 2.0 / head_size)
+    angles = positions.reshape(rows, 1).astype(F32) * freqs
+    cosine, sine = jnp.cos(angles), jnp.sin(angles)
+    cosine = jnp.concatenate([cosine, cosine], axis=-1).reshape(n, 8, head_size)
+    sine = jnp.concatenate([-sine, sine], axis=-1).reshape(n, 8, head_size)
+    x = hidden_in.reshape(rows, narrow)
+    struct = jax.ShapeDtypeStruct
+    whole, own = call(
+        functools.partial(project_kernel, n),
+        1,
+        [struct((3, depth, PLANE, 8, local_width), BF16), struct((3, 8, local_width), BF16)],
+        [
+            pltpu.VMEM((3, narrow, local_width), BF16),
+            pltpu.SemaphoreType.DMA((3,)),
+            pltpu.VMEM((n, 8, 128), F32),
+        ]
+        + pair(n - 1)
+        + sum_scratch(3, depth, local_width, F32)
+        + pipe_sems(3, depth),
+        x,
+        query_weight,
+        key_weight,
+        value_weight,
+        cosine,
+        sine,
+        far=(1, 2, 3),
+    )
+    group = 4
+    block = pl.BlockSpec((group, slot_count, local_width), lambda g: (g, 0, 0))
+    stat, acc, new_keys, new_values = pl.pallas_call(
+        functools.partial(cache_kernel, score_scale),
+        grid=(requests // group,),
+        out_shape=[
+            struct((rows, 128), F32),
+            struct((rows, local_width), F32),
+            struct(cache_keys.shape, BF16),
+            struct(cache_values.shape, BF16),
+        ],
+        in_specs=[
+            pl.BlockSpec(memory_space=pltpu.SMEM),
+            pl.BlockSpec((3, group // 2, 8, local_width), lambda g: (0, g, 0, 0)),
+            block,
+            block,
+        ],
+        out_specs=[
+            pl.BlockSpec((group * 4, 128), lambda g: (g, 0)),
+            pl.BlockSpec((group * 4, local_width), lambda g: (g, 0)),
+            block,
+            block,
+        ],
+    )(lengths, whole.reshape(3, n, 8, local_width), cache_keys, cache_values)
+    mixed, normed2 = call(
+        functools.partial(attend_kernel, n, score_scale),
+        2,
+        [struct((rows, narrow), F32), struct((rows, narrow), BF16)],
+        [
+            pltpu.VMEM((n, 8, 128), F32),
+            pltpu.VMEM((n, 8, 128), F32),
+            pltpu.VMEM((n, 8, 128), F32),
+            pltpu.VMEM((rows, narrow), F32),
+            pltpu.VMEM((rows, narrow), F32),
+        ]
+        + pair(n - 1)
+        + pair(n - 1)
+        + pair(1)
+        + sum_scratch(2, depth, local_width // 2 + 128, F32)
+        + [pltpu.VMEM((2, depth, PLANE, 8, local_width // 2), BF16)]
+        + pipe_sems(2, depth),
+        stat,
+        acc,
+        own,
+        x,
+        out_weight,
+    )
+    ff = gate_weight.shape[1]
+    chunks = ff // 1024
+    (block_out,) = call(
+        functools.partial(feed_kernel, n),
+        3,
+        [struct((rows, narrow), BF16)],
+        [pltpu.VMEM((rows, narrow), F32), pltpu.VMEM((rows, narrow), F32)]
+        + pair(1)
+        + sum_scratch(chunks, depth, 2 * ff // chunks, BF16)
+        + [pltpu.VMEM((chunks, depth, PLANE, 8, ff // chunks), BF16)]
+        + pipe_sems(chunks, depth),
+        normed2,
+        mixed,
+        gate_weight,
+        up_weight,
+        down_weight,
+    )
+    return block_out.reshape(requests, token_count, narrow), new_keys, new_values
+
+
+def body(n, model_shards, hidden_in, cache_keys, *rest):
+    rows = hidden_in.shape[0] * hidden_in.shape[1]
+    tiled = (
+        n % PLANE == 0
+        and rows == 128
+        and rows // n == 8
+        and hidden_in.shape[1] == 4
+        and hidden_in.shape[2] == 128
+        and cache_keys.shape[2] == 1024
+        and model_shards == 2
+    )
+    if tiled:
+        return body_kernels(n, hidden_in, cache_keys, *rest)
+    return body_plain(hidden_in, cache_keys, *rest)
+
+
 def solution(mesh):
     placed = (
         P(None, None, "seq"),
@@ -199,7 +746,7 @@
         P("mdl", "seq"),
     )
     return jax.shard_map(
-        body,
+        functools.partial(body, mesh.shape["seq"], mesh.shape["mdl"]),
         mesh=mesh,
         in_specs=placed,
         out_specs=(P(None, None, "seq"), P(None, "seq", "mdl"), P(None, "seq", "mdl")),

time: 623 us -> 148 us (0.24)
  waiting for transfers between devices: 319 us -> 0 us
  blocking collectives: 243 us -> 0 us
  Pallas kernels: 0 us -> 139 us
  matrix products: 31 us -> 0 us
  between operations: 14.1 us -> 0.75 us
  other arithmetic: 9.96 us -> 0.44 us
    psum x5 -> x0, waiting for transfers between devices: 319 us -> none  [the longest x1 160 us: body(): gate_full, up_full = lax.psum((gate_part, up_part), 'seq')]
    psum x3 -> x0, blocking collectives: 167 us -> none  [the longest x1 82 us: body(): lax.psum((query_part, key_part, value_part), 'seq')]
    pallas_call x0 -> x4, Pallas kernels: none -> 139 us  [the longest x3 121 us: call(): pl.pallas_call(kernel, out_shape=outs, in_specs=[pl.BlockSpec(memory_spac...]
    pmax x1 -> x0, blocking collectives: 75.7 us -> none  [body(): top_cache = lax.pmax(top_old, 'seq')]
    dot_general x13 -> x0, matrix products: 31 us -> none  [the longest x1 3.96 us: body(): jnp.einsum('rnf,fc->rnc', act_full, down_weight, preferred_element_type=j...]
  transfers between devices with their start and end apart: 5 -> 0, of which waited for: 5 -> 0; matrix products, arithmetic and copies ran while one was open for 2% -> 0% of each run, Pallas kernels for 0% -> 0%
where the time goes in v3:
time: 148 us
  Pallas kernels  139 us (94%)
  local copies, waits for them, and re-layouts  8.05 us (5%)
    pallas_call x3, Pallas kernels, call(): pl.pallas_call(kernel, out_shape=outs, in_specs=[pl.BlockSpec(memory_spac...  121 us
    pallas_call x1, Pallas kernels, body_kernels(): pl.pallas_call(functools.partial(cache_kernel, score_scale), grid=(reques...  17.4 us
    unnamed x25, local copies, waits for them, and re-layouts  7.01 us

profile of v3, /device:TPU:0, one launch (start us, length us, event | category | flops | bytes accessed | tf_op | source)
XLA Modules:
  0.0 148.0 jit_solution(9455134311337182503)
XLA Ops:
  0.6 0.7 add.24
  1.4 0.1 copy.17
  1.5 0.1 add.28
  1.5 0.1 copy.18
  1.6 0.1 copy.19
  1.7 0.3 fusion
  2.0 0.1 pad_maximum_fusion
  2.1 0.0 copy-start.6
  2.2 0.9 copy-done.6
  3.1 0.0 copy-start.7
  3.1 0.9 copy-done.7
  4.0 0.0 copy-start.8
  4.0 0.9 copy-done.8
  5.0 0.0 copy-start.9
  5.0 0.8 copy-done.9
  5.8 43.6 %shard_map.130 = (bf16[3,4,4,8,1024]{4,3,2,1,0:T(8,128)(2,1)S(1)}, bf16[3,8,1024]{2,1,0:T(8,128)(2,1)S(1)}) custom-call(bf16[128,128]{1,0:T(8,128)(2,1)S(1)} %bitcast.6, bf16[128,1024]{1,0:T(8,128)(2,1)S(1)} %copy-done.6, bf16[128,1024]{1,0:T(8,128)(2,1)S(1)} %copy-done.7, bf16[128,1024]{1,0:T(8,128)(2,1)S(1)} %copy-done.8, ...), custom_call_target="tpu_custom_call" | custom-call | tf_op jit(solution)/shard_map/pallas_call | solution.py:574
  49.4 0.0 copy-start.3
  49.4 0.9 copy-done.3
  50.3 0.0 copy-start.5
  50.3 0.0 copy-start.10
  50.3 0.0 copy-start
  50.3 0.0 copy-start.1
  50.3 0.0 copy-start.2
  50.3 17.4 %shard_map.131 = (f32[128,128]{1,0:T(8,128)}, f32[128,1024]{1,0:T(8,128)}, bf16[32,32,1024]{2,1,0:T(8,128)(2,1)}, bf16[32,32,1024]{2,1,0:T(8,128)(2,1)}) custom-call(s32[32]{0:T(128)} %len_ref.1, bf16[3,16,8,1024]{3,2,1,0:T(8,128)(2,1)} %bitcast.4, bf16[32,32,1024]{2,1,0:T(8,128)(2,1)} %k_ref.1, bf16[32,32,1024]{2,1,0:T(8,128)(2,1)} %v_ref.1), custom_call_target="tpu_custom_call" | custom-call | tf_op jit(solution)/shard_map/pallas_call | solution.py:653
  67.7 0.0 copy-done.5
  67.7 0.0 copy-done.10
  67.7 0.0 copy-start.4
  67.7 1.0 copy-done.4
  68.7 0.0 copy-start.11
  68.8 0.8 copy-done.11
  69.6 33.9 %shard_map.132 = (f32[128,128]{1,0:T(8,128)S(1)}, bf16[128,128]{1,0:T(8,128)(2,1)S(1)}) custom-call(f32[128,128]{1,0:T(8,128)S(1)} %copy-done.11, f32[128,1024]{1,0:T(8,128)S(1)} %copy-done.4, bf16[3,8,1024]{2,1,0:T(8,128)(2,1)S(1)} %get-tuple-element.14.own_ref, bf16[128,128]{1,0:T(8,128)(2,1)S(1)} %bitcast.7, bf16[1024,128]{1,0:T(8,128)(2,1)S(1)} %copy-done.5), custom_call_target="tpu_custom_call" | custom-call | tf_op jit(solution)/shard_map/pallas_call | solution.py:574
  103.4 0.0 copy-done
  103.5 0.0 copy-done.1
  103.5 0.0 copy-done.2
  103.5 43.9 %shard_map.133 = bf16[128,128]{1,0:T(8,128)(2,1)S(1)} custom-call(bf16[128,128]{1,0:T(8,128)(2,1)S(1)} %get-tuple-element.15.normed_ref, f32[128,128]{1,0:T(8,128)S(1)} %get-tuple-element.16.mixed_ref, bf16[128,4096]{1,0:T(8,128)(2,1)S(1)} %copy-done, bf16[128,4096]{1,0:T(8,128)(2,1)S(1)} %copy-done.1, bf16[4096,128]{1,0:T(8,128)(2,1)S(1)} %copy-done.2), custom_call_target="tpu_custom_call" | custom-call | tf_op jit(solution)/shard_map/pallas_call | solution.py:574
  147.4 0.6 copy.21
  (4 shorter events, 0.0 us)
Async XLA Ops:
  2.1 1.0 copy-start.6
  3.1 0.9 copy-start.7
  4.0 0.9 copy-start.8
  5.0 0.8 copy-start.9
  49.4 0.9 copy-start.3
  50.3 17.4 %copy-start.5 = (bf16[1024,128]{1,0:T(8,128)(2,1)S(1)}, bf16[1024,128]{1,0:T(8,128)(2,1)}, u32[]{:S(2)}) copy-start(bf16[1024,128]{1,0:T(8,128)(2,1)} %w_ref.1) | copy-start | bytes 786436
  50.3 17.4 %copy-start.10 = (bf16[32,4,128]{2,1,0:T(4,128)(2,1)S(1)}, bf16[32,4,128]{2,1,0:T(4,128)(2,1)}, u32[]{:S(2)}) copy-start(bf16[32,4,128]{2,1,0:T(4,128)(2,1)} %param.11) | copy-start | bytes 98308
  50.3 53.2 %copy-start = (bf16[128,4096]{1,0:T(8,128)(2,1)S(1)}, bf16[128,4096]{1,0:T(8,128)(2,1)}, u32[]{:S(2)}) copy-start(bf16[128,4096]{1,0:T(8,128)(2,1)} %wg.1) | copy-start | bytes 3145732
  50.3 53.2 %copy-start.1 = (bf16[128,4096]{1,0:T(8,128)(2,1)S(1)}, bf16[128,4096]{1,0:T(8,128)(2,1)}, u32[]{:S(2)}) copy-start(bf16[128,4096]{1,0:T(8,128)(2,1)} %wu.1) | copy-start | bytes 3145732
  50.3 53.2 %copy-start.2 = (bf16[4096,128]{1,0:T(8,128)(2,1)S(1)}, bf16[4096,128]{1,0:T(8,128)(2,1)}, u32[]{:S(2)}) copy-start(bf16[4096,128]{1,0:T(8,128)(2,1)} %wd.1) | copy-start | bytes 3145732
  67.7 1.0 copy-start.4
  68.7 0.8 copy-start.11

commit v4 on v3

--- a/solution.py
+++ b/solution.py
@@ -243,7 +243,7 @@
 
 
 def pipeline(
-    n, me, fill, finish, consume, part, got_plane, half, got_depth, whole, *sems
+    n, me, fill, launched, finish, consume, part, got_plane, half, got_depth, whole, *sems
 ):
     depth = n // PLANE
     chunks = part.shape[0]
@@ -267,6 +267,7 @@
                 c * (PLANE - 1) + j - 1,
                 peer,
             )
+    launched()
     for step in range(chunks + 3):
         c = step
         if c < chunks:
@@ -361,7 +362,18 @@
             own[c, :, i * 128 : (i + 1) * 128] = piece
 
     pipeline(
-        n, me, fill, finish, lambda c: None, part, got_plane, half, got_depth, whole, *rest[4:]
+        n,
+        me,
+        fill,
+        lambda: None,
+        finish,
+        lambda c: None,
+        part,
+        got_plane,
+        half,
+        got_depth,
+        whole,
+        *rest[4:],
     )
 
 
@@ -378,10 +390,10 @@
     for i in range(group):
         length = len_ref[step * group + i]
         at = (i % 2) * 4
-        fresh = [new_ref[c, i // 2].astype(F32) for c in range(3)]
+        fresh = new_ref[0, i // 2].astype(F32)
         keys, values = k_ref[i], v_ref[i]
         queries = jnp.concatenate(
-            [jnp.where(head_mask, fresh[0][at + t : at + t + 1], 0.0) for t in range(4)], axis=0
+            [jnp.where(head_mask, fresh[at + t : at + t + 1], 0.0) for t in range(4)], axis=0
         ).astype(BF16)
         scores = (
             lax.dot_general(queries, keys, (((1,), (1,)), ((), ())), preferred_element_type=F32)
@@ -410,21 +422,25 @@
                 axis=0,
                 keepdims=True,
             )
-        ko_ref[i] = keys
-        vo_ref[i] = values
-        first = length - base
+    for i in range(group):
+        ko_ref[i] = k_ref[i]
+        vo_ref[i] = v_ref[i]
+    for i in range(group):
+        first = len_ref[step * group + i] - base
+        at = (i % 2) * 4
 
         @pl.when((first < slots) & (first > -4))
         def _():
             place = lax.broadcasted_iota(jnp.int32, (slots, width), 0)
-            for rows, old, out in ((fresh[1], keys, ko_ref), (fresh[2], values, vo_ref)):
-                held = old.astype(F32)
+            for c, old, out in ((1, k_ref, ko_ref), (2, v_ref, vo_ref)):
+                rows = new_ref[c, i // 2].astype(F32)
+                held = old[i].astype(F32)
                 for t in range(4):
                     held = jnp.where(place == first + t, rows[at + t : at + t + 1], held)
                 out[i] = held.astype(BF16)
 
 
-def attend_kernel(
+def layer_kernel(
     n,
     scale,
     stat_ref,
@@ -432,8 +448,10 @@
     own_ref,
     x_ref,
     w_ref,
-    mixed_ref,
-    normed_ref,
+    wd,
+    wg,
+    wu,
+    out_ref,
     tops,
     slots,
     back_ref,
@@ -445,13 +463,50 @@
     recv,
     swap_send,
     swap_recv,
+    mixed_ref,
+    weights,
+    load_sem,
+    weight_send,
+    weight_recv,
+    normed_all,
+    normed_send,
+    normed_recv,
     *rest,
 ):
     me = lax.axis_index("seq")
     partner = 1 - lax.axis_index("mdl")
     enter(n, me, partner)
+    rest, feed = rest[:13], rest[13:]
     part, got_plane, half, got_depth, whole = rest[:5]
     rows = stat_ref.shape[0]
+    moves = []
+
+    def share_weights():
+        wide = weights.shape[-1]
+
+        def columns(w, q):
+            return w.at[:, pl.ds(pl.multiple_of(q * wide, wide), wide)]
+
+        for j in range(1, PLANE):
+            peer = plane_peer(me, j)
+            for i, w in enumerate((wg, wu)):
+                at = 2 * (j - 1) + i
+                moves.append(
+                    remote(
+                        columns(w, peer % PLANE),
+                        weights.at[me % PLANE, i],
+                        weight_send.at[at],
+                        weight_recv.at[at],
+                        {"seq": peer},
+                    )
+                )
+        for i, w in enumerate((wg, wu)):
+            load = pltpu.make_async_copy(
+                columns(w, me % PLANE), weights.at[me % PLANE, i], load_sem.at[i]
+            )
+            load.start()
+            moves.append(load)
+
     heads = acc_ref.shape[1] // 128
     chunks = part.shape[0]
     each = heads // chunks
@@ -513,56 +568,88 @@
         )
         mine[...] = made if c == 0 else mine[...] + made
 
-    pipeline(n, me, fill, finish, consume, *rest)
-    remote(mine, other, swap_send.at[0], swap_recv.at[0], {"mdl": partner}).wait()
-    mixed = x_ref[...].astype(F32) + (mine[...] + other[...])
+    pipeline(n, me, fill, share_weights, finish, consume, *rest)
+    remote(mine, other.at[0], swap_send.at[0], swap_recv.at[0], {"mdl": partner}).wait()
+    mixed = x_ref[...].astype(F32) + (mine[...] + other[0])
     mixed_ref[...] = mixed
-    normed_ref[...] = normalize_rows(mixed, *row_stats(n, me, mixed, slots, send, recv))
-
-
-def feed_kernel(
-    n,
-    normed_ref,
-    mixed_ref,
-    wg,
-    wu,
-    wd,
-    out_ref,
-    mine,
-    other,
-    swap_send,
-    swap_recv,
-    *rest,
-):
-    me = lax.axis_index("seq")
-    partner = 1 - lax.axis_index("mdl")
-    enter(n, me, partner)
-    part, got_plane, half, got_depth, whole = rest[:5]
-    rows = normed_ref.shape[0]
-    tile = whole.shape[-1]
-    normed = normed_ref[...]
-    shape = part.shape[1:4] + (tile,)
+    normed_all[p] = normalize_rows(mixed, *row_stats(n, me, mixed, slots, send, recv))
+    wait_all(
+        [
+            remote(
+                normed_all.at[p],
+                normed_all.at[p],
+                normed_send.at[j - 1],
+                normed_recv.at[j - 1],
+                {"seq": plane_peer(me, j)},
+            )
+            for j in range(1, PLANE)
+        ]
+    )
+    wait_all(moves)
+    feed_forward(n, me, normed_all, weights, wd, mine, *feed)
+    remote(mine, other.at[1], swap_send.at[1], swap_recv.at[1], {"mdl": partner}).wait()
+    out_ref[...] = (mixed_ref[...] + (mine[...] + other[1])).astype(BF16)
+
+
+def feed_forward(n, me, normed_all, weights, wd, total, part, got, whole, *sems):
+    depth = n // PLANE
     z, p = me // PLANE, me % PLANE
-
-    def fill(c):
-        for i, w in enumerate((wg, wu)):
-            made = jnp.dot(
-                normed, w[:, c * tile : (c + 1) * tile], preferred_element_type=F32
-            )
-            part[c, :, :, :, i * tile : (i + 1) * tile] = made.reshape(shape).astype(part.dtype)
-
-    def finish(c, sums):
-        gate, up = sums[:, :tile], sums[:, tile:]
-        whole[c, z, p] = (gate / (1.0 + jnp.exp(-gate)) * up).astype(BF16)
-
-    def consume(c):
-        act = whole[c].astype(F32).reshape(rows, tile).astype(BF16)
-        made = jnp.dot(act, wd[c * tile : (c + 1) * tile], preferred_element_type=F32)
-        mine[...] = made if c == 0 else mine[...] + made
-
-    pipeline(n, me, fill, finish, consume, *rest)
-    remote(mine, other, swap_send.at[0], swap_recv.at[0], {"mdl": partner}).wait()
-    out_ref[...] = (mixed_ref[...] + (mine[...] + other[...])).astype(BF16)
+    chunks = part.shape[0]
+    wide = weights.shape[-1]
+    tile = wide // chunks
+    rows = normed_all.shape[1]
+    flying = {}
+
+    def send(kind, c, src, dst, pair_at, peer):
+        flying.setdefault((kind, c), []).append(
+            remote(src, dst, sems[2 * kind].at[pair_at], sems[2 * kind + 1].at[pair_at], {"seq": peer})
+        )
+
+    for c in range(chunks):
+        for i in range(2):
+            made = jnp.zeros((rows, tile), F32)
+            for q in range(PLANE):
+                made = made + jnp.dot(
+                    normed_all[q],
+                    weights[q, i, :, c * tile : (c + 1) * tile],
+                    preferred_element_type=F32,
+                )
+            part[c, :, :, i * tile : (i + 1) * tile] = made.astype(part.dtype).reshape(
+                depth, rows // depth, tile
+            )
+        for k in range(1, depth):
+            peer = depth_peer(me, k, depth)
+            send(
+                0, c, part.at[c, peer // PLANE], got.at[c, k - 1], c * (depth - 1) + k - 1, peer
+            )
+    for step in range(chunks + 2):
+        c = step
+        if c < chunks:
+            wait_all(flying[0, c])
+            sums = part[c, z].astype(F32)
+            for k in range(depth - 1):
+                sums = sums + got[c, k].astype(F32)
+            gate, up = sums[:, :tile], sums[:, tile:]
+            whole[c, p, z] = (gate / (1.0 + jnp.exp(-gate)) * up).astype(BF16)
+            mine = whole.at[c, p, z]
+            for k in range(1, depth):
+                send(1, c, mine, mine, c * (depth - 1) + k - 1, depth_peer(me, k, depth))
+        c = step - 1
+        if 0 <= c < chunks:
+            wait_all(flying[1, c])
+            mine = whole.at[c, p]
+            for j in range(1, PLANE):
+                send(2, c, mine, mine, c * (PLANE - 1) + j - 1, plane_peer(me, j))
+        c = step - 2
+        if 0 <= c < chunks:
+            wait_all(flying[2, c])
+            for q in range(PLANE):
+                made = jnp.dot(
+                    whole[c, q].reshape(rows, tile),
+                    wd[q * wide + c * tile : q * wide + (c + 1) * tile],
+                    preferred_element_type=F32,
+                )
+                total[...] = made if c == 0 and q == 0 else total[...] + made
 
 
 def pair(count):
@@ -672,45 +759,50 @@
             block,
         ],
     )(lengths, whole.reshape(3, n, 8, local_width), cache_keys, cache_values)
-    mixed, normed2 = call(
-        functools.partial(attend_kernel, n, score_scale),
+    wide = gate_weight.shape[1] // PLANE
+    chunks = wide // 256
+    (block_out,) = call(
+        functools.partial(layer_kernel, n, score_scale),
         2,
-        [struct((rows, narrow), F32), struct((rows, narrow), BF16)],
+        [struct((rows, narrow), BF16)],
         [
             pltpu.VMEM((n, 8, 128), F32),
             pltpu.VMEM((n, 8, 128), F32),
             pltpu.VMEM((n, 8, 128), F32),
             pltpu.VMEM((rows, narrow), F32),
-            pltpu.VMEM((rows, narrow), F32),
+            pltpu.VMEM((2, rows, narrow), F32),
         ]
         + pair(n - 1)
         + pair(n - 1)
-        + pair(1)
+        + pair(2)
+        + [
+            pltpu.VMEM((rows, narrow), F32),
+            pltpu.VMEM((PLANE, 2, narrow, wide), BF16),
+            pltpu.SemaphoreType.DMA((2,)),
+        ]
+        + pair(2 * (PLANE - 1))
+        + [pltpu.VMEM((PLANE, rows, narrow), BF16)]
+        + pair(PLANE - 1)
         + sum_scratch(2, depth, local_width // 2 + 128, F32)
         + [pltpu.VMEM((2, depth, PLANE, 8, local_width // 2), BF16)]
-        + pipe_sems(2, depth),
+        + pipe_sems(2, depth)
+        + [
+            pltpu.VMEM((chunks, depth, rows // depth, 512), BF16),
+            pltpu.VMEM((chunks, depth - 1, rows // depth, 512), BF16),
+            pltpu.VMEM((chunks, PLANE, depth, rows // depth, 256), BF16),
+        ]
+        + pair(chunks * (depth - 1))
+        + pair(chunks * (depth - 1))
+        + pair(chunks * (PLANE - 1)),
         stat,
         acc,
         own,
         x,
         out_weight,
-    )
-    ff = gate_weight.shape[1]
-    chunks = ff // 1024
-    (block_out,) = call(
-        functools.partial(feed_kernel, n),
-        3,
-        [struct((rows, narrow), BF16)],
-        [pltpu.VMEM((rows, narrow), F32), pltpu.VMEM((rows, narrow), F32)]
-        + pair(1)
-        + sum_scratch(chunks, depth, 2 * ff // chunks, BF16)
-        + [pltpu.VMEM((chunks, depth, PLANE, 8, ff // chunks), BF16)]
-        + pipe_sems(chunks, depth),
-        normed2,
-        mixed,
+        down_weight,
         gate_weight,
         up_weight,
-        down_weight,
+        far=(6, 7),
     )
     return block_out.reshape(requests, token_count, narrow), new_keys, new_values
 

time: 148 us -> 145 us (0.980)
  Pallas kernels: 139 us -> 136 us
    pallas_call x1, Pallas kernels: 17.4 us -> 11.1 us  [body_kernels(): pl.pallas_call(functools.partial(cache_kernel, score_scale), grid=(reques...]
    pallas_call x3 -> x2, Pallas kernels: 121 us -> 125 us  [call(): pl.pallas_call(kernel, out_shape=outs, in_specs=[pl.BlockSpec(memory_spac...]
where the time goes in v4:
time: 145 us
  Pallas kernels  136 us (94%)
  local copies, waits for them, and re-layouts  8.06 us (6%)
    pallas_call x2, Pallas kernels, call(): pl.pallas_call(kernel, out_shape=outs, in_specs=[pl.BlockSpec(memory_spac...  125 us
    pallas_call x1, Pallas kernels, body_kernels(): pl.pallas_call(functools.partial(cache_kernel, score_scale), grid=(reques...  11.1 us
    unnamed x25, local copies, waits for them, and re-layouts  7.01 us

profile of v4, /device:TPU:0, one launch (start us, length us, event | category | flops | bytes accessed | tf_op | source)
XLA Modules:
  0.0 145.5 jit_solution(13761375523931731007)
XLA Ops:
  0.6 0.7 add.24
  1.4 0.1 copy.17
  1.5 0.1 add.28
  1.5 0.1 copy.18
  1.6 0.1 copy.19
  1.7 0.3 fusion
  2.0 0.1 pad_maximum_fusion
  2.1 0.0 copy-start.6
  2.2 0.9 copy-done.6
  3.1 0.0 copy-start.7
  3.1 0.9 copy-done.7
  4.0 0.0 copy-start.8
  4.0 0.9 copy-done.8
  5.0 0.0 copy-start.9
  5.0 0.8 copy-done.9
  5.8 43.6 %shard_map.130 = (bf16[3,4,4,8,1024]{4,3,2,1,0:T(8,128)(2,1)S(1)}, bf16[3,8,1024]{2,1,0:T(8,128)(2,1)S(1)}) custom-call(bf16[128,128]{1,0:T(8,128)(2,1)S(1)} %bitcast.6, bf16[128,1024]{1,0:T(8,128)(2,1)S(1)} %copy-done.6, bf16[128,1024]{1,0:T(8,128)(2,1)S(1)} %copy-done.7, bf16[128,1024]{1,0:T(8,128)(2,1)S(1)} %copy-done.8, ...), custom_call_target="tpu_custom_call" | custom-call | tf_op jit(solution)/shard_map/pallas_call | solution.py:661
  49.4 0.0 copy-start.3
  49.4 0.9 copy-done.3
  50.3 0.0 copy-start
  50.3 0.0 copy-start.1
  50.3 0.0 copy-start.2
  50.3 0.0 copy-start.5
  50.3 0.0 copy-start.10
  50.3 11.1 %shard_map.131 = (f32[128,128]{1,0:T(8,128)}, f32[128,1024]{1,0:T(8,128)}, bf16[32,32,1024]{2,1,0:T(8,128)(2,1)}, bf16[32,32,1024]{2,1,0:T(8,128)(2,1)}) custom-call(s32[32]{0:T(128)} %len_ref.1, bf16[3,16,8,1024]{3,2,1,0:T(8,128)(2,1)} %bitcast.4, bf16[32,32,1024]{2,1,0:T(8,128)(2,1)} %k_ref.1, bf16[32,32,1024]{2,1,0:T(8,128)(2,1)} %v_ref.1), custom_call_target="tpu_custom_call" | custom-call | tf_op jit(solution)/shard_map/pallas_call | solution.py:740
  61.4 0.0 copy-done
  61.4 0.0 copy-done.1
  61.4 0.0 copy-done.2
  61.4 0.0 copy-done.5
  61.4 0.0 copy-done.10
  61.5 0.0 copy-start.4
  61.5 1.0 copy-done.4
  62.5 0.0 copy-start.11
  62.5 0.8 copy-done.11
  63.3 81.5 %shard_map.132 = bf16[128,128]{1,0:T(8,128)(2,1)S(1)} custom-call(f32[128,128]{1,0:T(8,128)S(1)} %copy-done.11, f32[128,1024]{1,0:T(8,128)S(1)} %copy-done.4, bf16[3,8,1024]{2,1,0:T(8,128)(2,1)S(1)} %get-tuple-element.12.own_ref, bf16[128,128]{1,0:T(8,128)(2,1)S(1)} %bitcast.7, bf16[1024,128]{1,0:T(8,128)(2,1)S(1)} %copy-done.5, ...), custom_call_target="tpu_custom_call" | custom-call | tf_op jit(solution)/shard_map/pallas_call | solution.py:661
  144.8 0.6 copy.21
  (4 shorter events, 0.0 us)
Async XLA Ops:
  2.1 1.0 copy-start.6
  3.1 0.9 copy-start.7
  4.0 0.9 copy-start.8
  5.0 0.8 copy-start.9
  49.4 0.9 copy-start.3
  50.3 11.1 %copy-start = (bf16[4096,128]{1,0:T(8,128)(2,1)S(1)}, bf16[4096,128]{1,0:T(8,128)(2,1)}, u32[]{:S(2)}) copy-start(bf16[4096,128]{1,0:T(8,128)(2,1)} %wd.1) | copy-start | bytes 3145732
  50.3 11.1 %copy-start.1 = (bf16[128,4096]{1,0:T(8,128)(2,1)S(1)}, bf16[128,4096]{1,0:T(8,128)(2,1)}, u32[]{:S(2)}) copy-start(bf16[128,4096]{1,0:T(8,128)(2,1)} %wg.1) | copy-start | bytes 3145732
  50.3 11.1 %copy-start.2 = (bf16[128,4096]{1,0:T(8,128)(2,1)S(1)}, bf16[128,4096]{1,0:T(8,128)(2,1)}, u32[]{:S(2)}) copy-start(bf16[128,4096]{1,0:T(8,128)(2,1)} %wu.1) | copy-start | bytes 3145732
  50.3 11.1 %copy-start.5 = (bf16[1024,128]{1,0:T(8,128)(2,1)S(1)}, bf16[1024,128]{1,0:T(8,128)(2,1)}, u32[]{:S(2)}) copy-start(bf16[1024,128]{1,0:T(8,128)(2,1)} %w_ref.1) | copy-start | bytes 786436
  50.3 11.1 %copy-start.10 = (bf16[32,4,128]{2,1,0:T(4,128)(2,1)S(1)}, bf16[32,4,128]{2,1,0:T(4,128)(2,1)}, u32[]{:S(2)}) copy-start(bf16[32,4,128]{2,1,0:T(4,128)(2,1)} %param.11) | copy-start | bytes 98308
  61.5 1.0 copy-start.4
  62.5 0.8 copy-start.11

commit v5 on v3

--- a/solution.py
+++ b/solution.py
@@ -242,11 +242,15 @@
     )
 
 
+def chunk(refs, c):
+    return refs[c] if isinstance(refs, list) else refs.at[c]
+
+
 def pipeline(
     n, me, fill, finish, consume, part, got_plane, half, got_depth, whole, *sems
 ):
     depth = n // PLANE
-    chunks = part.shape[0]
+    chunks = len(part) if isinstance(part, list) else part.shape[0]
     z, p = me // PLANE, me % PLANE
     flying = {}
 
@@ -262,8 +266,8 @@
             send(
                 0,
                 c,
-                part.at[c, :, peer % PLANE],
-                got_plane.at[c, j - 1],
+                chunk(part, c).at[:, peer % PLANE],
+                chunk(got_plane, c).at[j - 1],
                 c * (PLANE - 1) + j - 1,
                 peer,
             )
@@ -272,26 +276,27 @@
         if c < chunks:
             wait_all(flying[0, c])
             for d in range(depth):
-                total = part[c, d, p].astype(F32)
+                total = chunk(part, c)[d, p].astype(F32)
                 for j in range(PLANE - 1):
-                    total = total + got_plane[c, j, d].astype(F32)
-                half[c, d] = total.astype(half.dtype)
+                    total = total + chunk(got_plane, c)[j, d].astype(F32)
+                mine = chunk(half, c)
+                mine[d] = total.astype(mine.dtype)
             for k in range(1, depth):
                 peer = depth_peer(me, k, depth)
                 send(
                     1,
                     c,
-                    half.at[c, peer // PLANE],
-                    got_depth.at[c, k - 1],
+                    chunk(half, c).at[peer // PLANE],
+                    chunk(got_depth, c).at[k - 1],
                     c * (depth - 1) + k - 1,
                     peer,
                 )
         c = step - 1
         if 0 <= c < chunks:
             wait_all(flying[1, c])
-            total = half[c, z].astype(F32)
+            total = chunk(half, c)[z].astype(F32)
             for k in range(depth - 1):
-                total = total + got_depth[c, k].astype(F32)
+                total = total + chunk(got_depth, c)[k].astype(F32)
             finish(c, total)
             for k in range(1, depth):
                 mine = whole.at[c, z, p]
@@ -341,7 +346,9 @@
     for load in loads:
         load.start()
     enter(n, me)
-    part, got_plane, half, got_depth = rest[:4]
+    part, got_plane, half, got_depth = (
+        [rest[i], rest[4 + i].at[0], rest[4 + i].at[1]] for i in range(4)
+    )
     widened = x_ref[...].astype(F32)
     normed = normalize_rows(widened, *row_stats(n, me, widened, slots, send, recv))
     z, p = me // PLANE, me % PLANE
@@ -349,7 +356,7 @@
     def fill(c):
         loads[c].wait()
         made = jnp.dot(normed, held[c], preferred_element_type=F32)
-        part[c] = made.reshape(part.shape[1:])
+        part[c][...] = made.reshape(part[c].shape).astype(part[c].dtype)
 
     def finish(c, sums):
         for i in range(sums.shape[1] // 128):
@@ -361,7 +368,7 @@
             own[c, :, i * 128 : (i + 1) * 128] = piece
 
     pipeline(
-        n, me, fill, finish, lambda c: None, part, got_plane, half, got_depth, whole, *rest[4:]
+        n, me, fill, finish, lambda c: None, part, got_plane, half, got_depth, whole, *rest[8:]
     )
 
 
@@ -378,10 +385,10 @@
     for i in range(group):
         length = len_ref[step * group + i]
         at = (i % 2) * 4
-        fresh = [new_ref[c, i // 2].astype(F32) for c in range(3)]
+        fresh = new_ref[0, i // 2].astype(F32)
         keys, values = k_ref[i], v_ref[i]
         queries = jnp.concatenate(
-            [jnp.where(head_mask, fresh[0][at + t : at + t + 1], 0.0) for t in range(4)], axis=0
+            [jnp.where(head_mask, fresh[at + t : at + t + 1], 0.0) for t in range(4)], axis=0
         ).astype(BF16)
         scores = (
             lax.dot_general(queries, keys, (((1,), (1,)), ((), ())), preferred_element_type=F32)
@@ -410,15 +417,19 @@
                 axis=0,
                 keepdims=True,
             )
-        ko_ref[i] = keys
-        vo_ref[i] = values
-        first = length - base
+    for i in range(group):
+        ko_ref[i] = k_ref[i]
+        vo_ref[i] = v_ref[i]
+    for i in range(group):
+        first = len_ref[step * group + i] - base
+        at = (i % 2) * 4
 
         @pl.when((first < slots) & (first > -4))
         def _():
             place = lax.broadcasted_iota(jnp.int32, (slots, width), 0)
-            for rows, old, out in ((fresh[1], keys, ko_ref), (fresh[2], values, vo_ref)):
-                held = old.astype(F32)
+            for c, old, out in ((1, k_ref, ko_ref), (2, v_ref, vo_ref)):
+                rows = new_ref[c, i // 2].astype(F32)
+                held = old[i].astype(F32)
                 for t in range(4):
                     held = jnp.where(place == first + t, rows[at + t : at + t + 1], held)
                 out[i] = held.astype(BF16)
@@ -638,7 +649,10 @@
             pltpu.VMEM((n, 8, 128), F32),
         ]
         + pair(n - 1)
-        + sum_scratch(3, depth, local_width, F32)
+        + [
+            pltpu.VMEM(ref.shape[1:], F32) for ref in sum_scratch(1, depth, local_width, F32)
+        ]
+        + sum_scratch(2, depth, local_width, BF16)
         + pipe_sems(3, depth),
         x,
         query_weight,

time: 148 us -> 137 us (0.926)
  Pallas kernels: 139 us -> 127 us
    pallas_call x1, Pallas kernels: 17.4 us -> 10.9 us  [body_kernels(): pl.pallas_call(functools.partial(cache_kernel, score_scale), grid=(reques...]
    pallas_call x3, Pallas kernels: 121 us -> 117 us  [call(): pl.pallas_call(kernel, out_shape=outs, in_specs=[pl.BlockSpec(memory_spac...]
where the time goes in v5:
time: 137 us
  Pallas kernels  127 us (93%)
  local copies, waits for them, and re-layouts  8.05 us (6%)
    pallas_call x3, Pallas kernels, call(): pl.pallas_call(kernel, out_shape=outs, in_specs=[pl.BlockSpec(memory_spac...  117 us
    pallas_call x1, Pallas kernels, body_kernels(): pl.pallas_call(functools.partial(cache_kernel, score_scale), grid=(reques...  10.9 us
    unnamed x25, local copies, waits for them, and re-layouts  7.01 us

profile of v5, /device:TPU:0, one launch (start us, length us, event | category | flops | bytes accessed | tf_op | source)
XLA Modules:
  0.0 136.7 jit_solution(12662479947082810658)
XLA Ops:
  0.6 0.7 add.24
  1.4 0.1 copy.17
  1.5 0.1 add.28
  1.5 0.1 copy.18
  1.6 0.1 copy.19
  1.7 0.3 fusion
  2.0 0.1 pad_maximum_fusion
  2.1 0.0 copy-start.6
  2.2 0.9 copy-done.6
  3.1 0.0 copy-start.7
  3.1 0.9 copy-done.7
  4.0 0.0 copy-start.8
  4.0 0.9 copy-done.8
  5.0 0.0 copy-start.9
  5.0 0.8 copy-done.9
  5.8 38.7 %shard_map.130 = (bf16[3,4,4,8,1024]{4,3,2,1,0:T(8,128)(2,1)S(1)}, bf16[3,8,1024]{2,1,0:T(8,128)(2,1)S(1)}) custom-call(bf16[128,128]{1,0:T(8,128)(2,1)S(1)} %bitcast.6, bf16[128,1024]{1,0:T(8,128)(2,1)S(1)} %copy-done.6, bf16[128,1024]{1,0:T(8,128)(2,1)S(1)} %copy-done.7, bf16[128,1024]{1,0:T(8,128)(2,1)S(1)} %copy-done.8, ...), custom_call_target="tpu_custom_call" | custom-call | tf_op jit(solution)/shard_map/pallas_call | solution.py:585
  44.5 0.0 copy-start.3
  44.5 0.9 copy-done.3
  45.4 0.0 copy-start.5
  45.4 0.0 copy-start.10
  45.4 0.0 copy-start
  45.4 0.0 copy-start.1
  45.4 0.0 copy-start.2
  45.4 10.9 %shard_map.131 = (f32[128,128]{1,0:T(8,128)}, f32[128,1024]{1,0:T(8,128)}, bf16[32,32,1024]{2,1,0:T(8,128)(2,1)}, bf16[32,32,1024]{2,1,0:T(8,128)(2,1)}) custom-call(s32[32]{0:T(128)} %len_ref.1, bf16[3,16,8,1024]{3,2,1,0:T(8,128)(2,1)} %bitcast.4, bf16[32,32,1024]{2,1,0:T(8,128)(2,1)} %k_ref.1, bf16[32,32,1024]{2,1,0:T(8,128)(2,1)} %v_ref.1), custom_call_target="tpu_custom_call" | custom-call | tf_op jit(solution)/shard_map/pallas_call | solution.py:667
  56.3 0.0 copy-done.5
  56.3 0.0 copy-done.10
  56.3 0.0 copy-start.4
  56.3 1.0 copy-done.4
  57.3 0.0 copy-start.11
  57.3 0.8 copy-done.11
  58.2 34.3 %shard_map.132 = (f32[128,128]{1,0:T(8,128)S(1)}, bf16[128,128]{1,0:T(8,128)(2,1)S(1)}) custom-call(f32[128,128]{1,0:T(8,128)S(1)} %copy-done.11, f32[128,1024]{1,0:T(8,128)S(1)} %copy-done.4, bf16[3,8,1024]{2,1,0:T(8,128)(2,1)S(1)} %get-tuple-element.14.own_ref, bf16[128,128]{1,0:T(8,128)(2,1)S(1)} %bitcast.7, bf16[1024,128]{1,0:T(8,128)(2,1)S(1)} %copy-done.5), custom_call_target="tpu_custom_call" | custom-call | tf_op jit(solution)/shard_map/pallas_call | solution.py:585
  92.5 0.0 copy-done
  92.5 0.0 copy-done.1
  92.5 0.0 copy-done.2
  92.5 43.6 %shard_map.133 = bf16[128,128]{1,0:T(8,128)(2,1)S(1)} custom-call(bf16[128,128]{1,0:T(8,128)(2,1)S(1)} %get-tuple-element.15.normed_ref, f32[128,128]{1,0:T(8,128)S(1)} %get-tuple-element.16.mixed_ref, bf16[128,4096]{1,0:T(8,128)(2,1)S(1)} %copy-done, bf16[128,4096]{1,0:T(8,128)(2,1)S(1)} %copy-done.1, bf16[4096,128]{1,0:T(8,128)(2,1)S(1)} %copy-done.2), custom_call_target="tpu_custom_call" | custom-call | tf_op jit(solution)/shard_map/pallas_call | solution.py:585
  136.1 0.6 copy.21
  (4 shorter events, 0.0 us)
Async XLA Ops:
  2.1 1.0 copy-start.6
  3.1 0.9 copy-start.7
  4.0 0.9 copy-start.8
  5.0 0.8 copy-start.9
  44.5 0.9 copy-start.3
  45.4 10.9 %copy-start.5 = (bf16[1024,128]{1,0:T(8,128)(2,1)S(1)}, bf16[1024,128]{1,0:T(8,128)(2,1)}, u32[]{:S(2)}) copy-start(bf16[1024,128]{1,0:T(8,128)(2,1)} %w_ref.1) | copy-start | bytes 786436
  45.4 10.9 %copy-start.10 = (bf16[32,4,128]{2,1,0:T(4,128)(2,1)S(1)}, bf16[32,4,128]{2,1,0:T(4,128)(2,1)}, u32[]{:S(2)}) copy-start(bf16[32,4,128]{2,1,0:T(4,128)(2,1)} %param.11) | copy-start | bytes 98308
  45.4 47.1 %copy-start = (bf16[128,4096]{1,0:T(8,128)(2,1)S(1)}, bf16[128,4096]{1,0:T(8,128)(2,1)}, u32[]{:S(2)}) copy-start(bf16[128,4096]{1,0:T(8,128)(2,1)} %wg.1) | copy-start | bytes 3145732
  45.4 47.1 %copy-start.1 = (bf16[128,4096]{1,0:T(8,128)(2,1)S(1)}, bf16[128,4096]{1,0:T(8,128)(2,1)}, u32[]{:S(2)}) copy-start(bf16[128,4096]{1,0:T(8,128)(2,1)} %wu.1) | copy-start | bytes 3145732
  45.4 47.1 %copy-start.2 = (bf16[4096,128]{1,0:T(8,128)(2,1)S(1)}, bf16[4096,128]{1,0:T(8,128)(2,1)}, u32[]{:S(2)}) copy-start(bf16[4096,128]{1,0:T(8,128)(2,1)} %wd.1) | copy-start | bytes 3145732
  56.3 1.0 copy-start.4
  57.3 0.8 copy-start.11
